TPU v7x, 128 devices: a whole 4x4x4 slice. The times are simulated.
128 devices in a mesh: dp: 16 (over x, z), tensor: 8 (over y, core).
Axes of the slice: x: 4, y: 4, z: 4, core: 2. Of those that a mesh axis runs over, the one named last changes fastest.
Arguments:
- activations: bfloat16 [256, 256, 14336], P('dp', None, 'tensor'), may hold values from -6 to 6
- out_grads: bfloat16 [256, 256, 4096], P('dp', None, 'tensor'), may hold values from -0.29882812 to 0.29882812
- lengths: int32 [256], P('dp'), may hold values from 1 to 256, 49152 in all
- bank_in: bfloat16 [16, 128, 64], replicated, may hold values from -0.046875 to 0.046875
- index_in: int32 [112], P('tensor'), may hold values from 0 to 15
- bank_out: bfloat16 [16, 128, 64], replicated, may hold values from -0.09375 to 0.09375
- index_out: int32 [32], P('tensor'), may hold values from 0 to 15
- prior_cov: float32 [4096, 4096], P('dp'), may hold values from -1 to 5, as said below
- val_grads: float32 [4096, 512], P('dp', 'tensor'), may hold values from -0.3 to 0.3
Outputs:
- scores: float32 [256, 512], P('dp', 'tensor')
Inputs may be any that keep to these rules, and one draw needn't show every extreme that they name: `lengths`: the longest rollout uses all 256 slots. `prior_cov`: symmetric and positive definite.
All inputs are finite; a program needn't handle non-finite values. No bound on the sum of `lengths` on one device may be relied on, other than what follows from the above.
Results may differ from a plain program's by a relative error of at most 0.0003.
Values sent between devices are 32-bit elements; how exact they have to be, the bound alone decides.
No kernel may reach another device: no remote copies, remote signals or barrier semaphores. Data moves between devices by JAX's collectives and lax.ppermute only.
A program may use at most 128 MiB of HBM per device.

v0:
```python
import functools

import jax
import jax.numpy as jnp
from jax import lax
from jax.experimental import pallas as pl
from jax.experimental.pallas import tpu as pltpu
from jax.sharding import PartitionSpec as P

ITERS = 6
F32 = jnp.float32
BF16 = jnp.bfloat16
HIGHEST = lax.Precision.HIGHEST

NT = (((1,), (1,)), ((), ()))
NN = (((1,), (0,)), ((), ()))
TN = (((0,), (0,)), ((), ()))

SIDE = 4
CORES = 2
BLK = 256
SEG = 32
OWN = 512
COLS = 32
VMEM = pl.BlockSpec(memory_space=pltpu.VMEM)
SMEM = pl.BlockSpec(memory_space=pltpu.SMEM)
HBM = pl.BlockSpec(memory_space=pltpu.HBM)


def params(mib):
    return pltpu.CompilerParams(vmem_limit_bytes=mib << 20)


def in_vmem(values):
    return [pltpu.with_memory_space_constraint(v, pltpu.VMEM) for v in values]


def in_hbm(values):
    return [pltpu.with_memory_space_constraint(v, pltpu.HBM) for v in values]


def place():
    dp = lax.axis_index("dp").astype(jnp.int32)
    tensor = lax.axis_index("tensor").astype(jnp.int32)
    return lax.div(dp, SIDE), lax.rem(dp, SIDE), dp, lax.div(tensor, CORES), lax.rem(tensor, CORES)


def fetch(sources, targets, sems):
    copies = [pltpu.make_async_copy(a, b, sems.at[i]) for i, (a, b) in enumerate(zip(sources, targets))]
    for copy in copies:
        copy.start()
    return copies


def cost(flops, nbytes):
    return pl.CostEstimate(flops=flops, bytes_accessed=nbytes, transcendentals=0)


def split(value):
    high = value.astype(BF16)
    return high, (value - high.astype(F32)).astype(BF16)


def mm(a, b, dims):
    return lax.dot_general(a, b, dims, preferred_element_type=F32)


def mm3(a, b, dims):
    return mm(a[0], b[0], dims) + mm(a[1], b[0], dims) + mm(a[0], b[1], dims)


def along_z(step):
    return [(i, (i // SIDE) * SIDE + (i + step) % SIDE) for i in range(16)]


def along_x(step):
    return [(i, (i + step * SIDE) % 16) for i in range(16)]


def along_y(step):
    return [(i, (i + step * CORES) % 8) for i in range(8)]


def other_core():
    return [(i, i ^ 1) for i in range(8)]


ORDER = ("zxy", "yzx")


def shifted(step, stage):
    pairs = []
    for dp in range(16):
        for tensor in range(8):
            axis = ORDER[tensor % CORES][stage]
            to_dp = {"x": along_x, "z": along_z}[axis](step)[dp][1] if axis != "y" else dp
            to_tensor = along_y(step)[tensor][1] if axis == "y" else tensor
            pairs.append((dp * 8 + tensor, to_dp * 8 + to_tensor))
    return pairs


def project_kernel(
    idx_in, idx_out, act, grad, bank_in, bank_out, out, acts, grads, proj_in, proj_out, sems, *, flip
):
    _, _, _, y, core = place()
    side = 1 - core if flip else core
    copies = []
    for i, (index, bank, proj) in enumerate(((idx_in, bank_in, proj_in), (idx_out, bank_out, proj_out))):
        blocks = proj.shape[1] // 128
        copies.append(
            fetch(
                [bank.at[index[b]] for b in range(blocks)],
                [proj.at[:, pl.ds(b * 128, 128)] for b in range(blocks)],
                sems.at[pl.ds(16 + 14 * i, blocks)],
            )
        )
    rolls = [side * 8 + lax.rem(y + j // 2, SIDE) * 2 + j % 2 for j in range(8)]
    blocks = []
    for j in range(8):
        blocks.append(fetch((act.at[rolls[j]], grad.at[rolls[j]]), (acts.at[j], grads.at[j]), sems.at[pl.ds(2 * j, 2)]))
    for group in copies:
        for copy in group:
            copy.wait()
    for j in range(8):
        for copy in blocks[j]:
            copy.wait()
        out[j, :, 0:64] = mm(acts[j], proj_in[...], NT)
        out[j, :, 64:128] = mm(grads[j], proj_out[...], NT)


def project(idx_in, idx_out, act, grad, bank_in_t, bank_out_t, flip):
    slots, width, model = act.shape[1], act.shape[2], grad.shape[2]
    return pl.pallas_call(
        functools.partial(project_kernel, flip=flip),
        out_shape=jax.ShapeDtypeStruct((8, slots, 128), F32),
        in_specs=[SMEM] * 2 + [HBM] * 4,
        out_specs=VMEM,
        scratch_shapes=[
            pltpu.VMEM((8, slots, width), BF16), pltpu.VMEM((8, slots, model), BF16),
            pltpu.VMEM((64, width), BF16), pltpu.VMEM((64, model), BF16),
            pltpu.SemaphoreType.DMA((34,)),
        ],
        compiler_params=params(20),
        cost_estimate=cost(16 * slots * (width + model) * 256, 16 * slots * (width + model)),
        name="project",
    )(idx_in, idx_out, *in_hbm([act, grad, bank_in_t, bank_out_t]))


def slab_kernel(prior, out, rows, sems):
    _, _, _, y, core = place()
    first = (y * CORES + core) * SEG
    parts = [pl.ds(i * 8, 8) for i in range(SEG // 8)]
    reads = fetch(
        [prior.at[pl.ds(pl.multiple_of(first + i * 8, 8), 8)] for i in range(SEG // 8)],
        [rows.at[p] for p in parts], sems,
    )
    writes = []
    for i, read in enumerate(reads):
        read.wait()
        writes += fetch([rows.at[parts[i]]], [out.at[parts[i]]], sems.at[pl.ds(SEG // 8 + i, 1)])
    for write in writes:
        write.wait()


def own_slab(prior):
    shape = (SEG, prior.shape[1])
    return pl.pallas_call(
        slab_kernel,
        out_shape=pltpu.HBM(shape, F32),
        in_specs=[HBM],
        out_specs=HBM,
        scratch_shapes=[pltpu.VMEM(shape, F32), pltpu.SemaphoreType.DMA((SEG // 4,))],
        name="own_slab",
    )(*in_hbm([prior]))


def factor_kernel(lens, v0, v1, w1, w2, w3, out):
    _, _, _, y, core = place()
    slots = v0.shape[1]
    for r in range(2):
        total = (v0[r] + v1[r]) + (w1[r] + w2[r]) + w3[r]
        used = lax.broadcasted_iota(jnp.int32, (slots, 64), 0) < lens[core * 8 + y * 2 + r]
        grad = jnp.where(used, total[:, 64:128], 0.0)
        out[r] = mm3(split(grad), split(total[:, 0:64]), TN)


def factor(lens, pieces):
    return pl.pallas_call(
        factor_kernel,
        out_shape=jax.ShapeDtypeStruct((2, 64, 64), F32),
        in_specs=[SMEM] + [VMEM] * 5,
        out_specs=VMEM,
        name="factor",
    )(lens, *in_vmem(pieces))


def rowsum(value):
    return jnp.sum(value, axis=1, keepdims=True)


def put(stack, cols, value):
    half = stack.shape[0] // 2
    stack[0:half, cols], stack[half:, cols] = split(value)


def loop(count, body, carry=None):
    return lax.fori_loop(0, count, body, carry)


def part_at(i, size):
    return pl.ds(pl.multiple_of(i * size, size), size)


def against_prior(stack, hi, lo, out):
    half = stack.shape[0] // 2

    def rows(i, carry):
        at = part_at(i, 256)
        both = mm(stack[...], hi[at, :], NT)
        out[0:half, at] = both[0:half] + both[half:] + mm(stack[0:half, :], lo[at, :], NT)
        return carry

    loop(hi.shape[0] // 256, rows)


def against_factors(stack, hi, lo):
    half = stack.shape[0] // 2
    size = hi.shape[1] // 2

    def chunk(i, acc):
        at = part_at(i, size)
        both = mm(stack[:, at], hi[:, at], NT)
        return acc + both[0:half] + both[half:] + mm(stack[0:half, at], lo[:, at], NT)

    return loop(2, chunk, jnp.zeros((half, hi.shape[0]), F32))


BLOCKS = [slice(k * BLK, (k + 1) * BLK) for k in range(16)]


def start_kernel(b0, b1, b2, b3, start, stack, pieces, sems):
    begin = fetch((b0, b1, b2, b3), [pieces.at[i] for i in range(4)], sems)
    _, _, _, y, _ = place()
    for d in range(SIDE):
        begin[d].wait()
        at = pl.ds(pl.multiple_of(lax.rem(y + SIDE - d, SIDE) * 8, 8), 8)
        for i in range(16):
            start[at, BLOCKS[i]] = pieces[d, i]
    for cols in BLOCKS:
        put(stack, cols, start[:, cols])


def assemble_start(pieces, n):
    sds = jax.ShapeDtypeStruct
    return pl.pallas_call(
        start_kernel,
        out_shape=(sds((COLS, n), F32), sds((2 * COLS, n), BF16)),
        in_specs=[HBM] * 4,
        out_specs=(VMEM, VMEM),
        scratch_shapes=[pltpu.VMEM((4, 16, 8, BLK), F32), pltpu.SemaphoreType.DMA((4,))],
        compiler_params=params(12),
        name="assemble_start",
    )(*in_hbm(pieces))


def prior_kernel(stack, prior_hbm, pri_hi, pri_lo, out, prior, sems):
    pieces = [pl.ds(i * SEG, SEG) for i in range(16)]
    fetch([prior_hbm.at[p] for p in pieces], [prior.at[p] for p in pieces], sems)
    _, _, _, y, core = place()
    t = y * CORES + core
    on_diag = lax.broadcasted_iota(jnp.int32, (SEG, 128), 1) == lax.rem(t, 4) * SEG + lax.broadcasted_iota(jnp.int32, (SEG, 128), 0)

    def piece(i, diag):
        rows = part_at(i, SEG)
        pltpu.make_async_copy(prior_hbm.at[rows], prior.at[rows], sems.at[i]).wait()
        for cols in BLOCKS:
            pri_hi[rows, cols], pri_lo[rows, cols] = split(prior[rows, cols])
        at = pl.ds(pl.multiple_of(i * BLK + lax.div(t, 4) * 128, 128), 128)
        return diag + jnp.where(on_diag, prior[rows, at], 0.0)

    diag = loop(16, piece, jnp.zeros((SEG, 128), F32))
    against_prior(stack, pri_hi, pri_lo, out)
    out[COLS : COLS + 8, :] = jnp.full((8, OWN), jnp.sum(diag), F32)


def prior_image(stack, prior):
    n = prior.shape[1]
    return pl.pallas_call(
        prior_kernel,
        out_shape=(
            pltpu.VMEM((OWN, n), BF16), pltpu.VMEM((OWN, n), BF16), jax.ShapeDtypeStruct((COLS + 8, OWN), F32),
        ),
        in_specs=[VMEM, HBM],
        out_specs=(VMEM,) * 3,
        scratch_shapes=[pltpu.VMEM((OWN, n), F32), pltpu.SemaphoreType.DMA((16,))],
        compiler_params=params(28),
        cost_estimate=cost(6 * 256 * OWN * n, 8 * OWN * n),
        name="prior_image",
    )(stack, *in_hbm([prior]))


def low_rank(stack, f_hi, f_lo, query, low):
    q = against_factors(stack, f_hi, f_lo)
    query[...] = q
    parts = split(q * (1.0 / f_hi.shape[0]))

    def columns(i, carry):
        for k in range(4):
            at = part_at(4 * i + k, BLK)
            low[:, at] = mm3(parts, (f_hi[:, at], f_lo[:, at]), NN)
        return carry

    loop(4, columns)


def factors_kernel(n0, n1, n2, n3, m0, m1, m2, m3, stack, f_hi, f_lo, query, low, square_out, pieces, sems):
    copies = fetch((n0, n1, n2, n3, m0, m1, m2, m3), [pieces.at[i] for i in range(8)], sems)
    square = jnp.zeros((32, BLK), F32)
    for i in range(8):
        copies[i].wait()
        rows = slice(i * 32, (i + 1) * 32)
        for cols in BLOCKS:
            value = pieces[i, :, cols]
            square = square + value * value
            f_hi[rows, cols], f_lo[rows, cols] = split(value)
    square_out[...] = jnp.full(square_out.shape, jnp.sum(square), F32)
    low_rank(stack, f_hi, f_lo, query, low)


def take_factors(pieces, stack):
    n = stack.shape[1]
    sds = jax.ShapeDtypeStruct
    return pl.pallas_call(
        factors_kernel,
        out_shape=(
            pltpu.VMEM((256, n), BF16), pltpu.VMEM((256, n), BF16),
            sds((COLS, 256), F32), sds((COLS, n), F32), sds((8, 128), F32),
        ),
        in_specs=[HBM] * 8 + [VMEM],
        out_specs=(VMEM,) * 5,
        scratch_shapes=[pltpu.VMEM((8, 32, n), F32), pltpu.SemaphoreType.DMA((8,))],
        compiler_params=params(20),
        cost_estimate=cost(12 * 256 * 256 * n, 8 * 256 * n),
        name="take_factors",
    )(*in_hbm(pieces), stack)


def low_rank_step(stack, f_hi, f_lo):
    n = stack.shape[1]
    sds = jax.ShapeDtypeStruct
    return pl.pallas_call(
        low_rank,
        out_shape=(sds((COLS, 256), F32), sds((COLS, n), F32)),
        in_specs=[VMEM] * 3,
        out_specs=(VMEM,) * 2,
        compiler_params=params(16),
        cost_estimate=cost(12 * 256 * 256 * n, 4 * 256 * n),
        name="low_rank",
    )(stack, f_hi, f_lo)


def arrange(mine, theirs, perm, image):
    _, _, _, y, core = place()
    for d in range(SIDE):
        chip = lax.rem(y + SIDE - d, SIDE) * CORES
        for side, line in ((core, mine), (1 - core, theirs)):
            at = pl.ds(pl.multiple_of((chip + side) * OWN, OWN), OWN)
            perm[:, at] = line[0:COLS, d * OWN : (d + 1) * OWN]
    lane = lax.broadcasted_iota(jnp.int32, (COLS, 128), 1)
    low64 = lane < 64
    even = lax.rem(lane // SEG, 2) == 0
    for high in range(2):
        for g in range(4):
            x = [perm[:, pl.ds(((4 * high + k) * 4 + g) * 128, 128)] for k in range(4)]
            rolled = [pltpu.roll(v, 64, 1) for v in x]
            a0 = jnp.where(low64, x[0], rolled[2])
            a2 = jnp.where(low64, rolled[0], x[2])
            a1 = jnp.where(low64, x[1], rolled[3])
            a3 = jnp.where(low64, rolled[1], x[3])
            result = (
                jnp.where(even, a0, pltpu.roll(a1, SEG, 1)), jnp.where(even, pltpu.roll(a0, 128 - SEG, 1), a1),
                jnp.where(even, a2, pltpu.roll(a3, SEG, 1)), jnp.where(even, pltpu.roll(a2, 128 - SEG, 1), a3),
            )
            for m in range(4):
                first = (4 * g + m) * BLK + high * 128
                image[:, first : first + 128] = result[m]


def own_part(direc):
    _, _, _, y, core = place()
    t = y * CORES + core
    group = lax.broadcasted_iota(jnp.int32, (COLS, 128), 1) // SEG
    parts = []
    for g in range(4):
        value = jnp.zeros((COLS, 128), F32)
        for m in range(4):
            at = pl.ds(pl.multiple_of((4 * g + m) * BLK + lax.div(t, 4) * 128, 128), 128)
            moved = pltpu.roll(direc[:, at], lax.rem((m + 4 - lax.rem(t, 4)) * SEG, 128), 1)
            value = jnp.where(group == m, moved, value)
        parts.append(value)
    return jnp.concatenate(parts, axis=1)


def step_body(pieces, damping, norm, res_in, direc_in, low, query, pri_hi, pri_lo, out, res, direc, stack, perm, image):
    arrange(*pieces, perm, image)
    curve = jnp.zeros((COLS, 1), F32)
    for cols in BLOCKS:
        old = direc_in[:, cols]
        value = image[:, cols] + low[:, cols] + damping * old
        image[:, cols] = value
        curve = curve + rowsum(old * value)
    if norm is None:
        norm = jnp.zeros((COLS, 1), F32)
        for cols in BLOCKS:
            norm = norm + rowsum(res_in[:, cols] * res_in[:, cols])
    alpha = norm / curve
    fresh = jnp.zeros((COLS, 1), F32)
    for cols in BLOCKS:
        value = res_in[:, cols] - alpha * image[:, cols]
        res[:, cols] = value
        fresh = fresh + rowsum(value * value)
    beta = fresh / norm
    for cols in BLOCKS:
        value = res[:, cols] + beta * direc_in[:, cols]
        direc[:, cols] = value
        put(stack, cols, value)
    against_prior(stack, pri_hi, pri_lo, out)
    return alpha, fresh


def first_kernel(
    mine, theirs, start, low, query, square, pri_hi, pri_lo,
    res, direc, stack_out, rr, score, damp, out, stack, perm, image,
):
    pieces = (mine, theirs)
    trace = square[0:1, 0:1] * (1.0 / query.shape[1])
    for piece in pieces:
        for d in range(SIDE):
            trace = trace + piece[COLS : COLS + 1, d * OWN : d * OWN + 1]
    damping = 0.1 * trace / start.shape[1]
    damp[...] = jnp.broadcast_to(damping, damp.shape)
    alpha, fresh = step_body(
        pieces, damping, None, start, start, low, query, pri_hi, pri_lo, out, res, direc, stack, perm, image
    )
    stack_out[...] = stack[...]
    rr[...] = jnp.broadcast_to(fresh, rr.shape)
    score[...] = alpha * query[...]


def step_kernel(
    mine, theirs, res_in, direc_in, rr_in, score_in, damp, low, query, pri_hi, pri_lo,
    res, direc, stack_out, rr, score, out, stack, perm, image,
):
    alpha, fresh = step_body(
        (mine, theirs), damp[0:1, 0:1], rr_in[:, 0:1], res_in, direc_in, low, query, pri_hi, pri_lo,
        out, res, direc, stack, perm, image,
    )
    stack_out[...] = stack[...]
    rr[...] = jnp.broadcast_to(fresh, rr.shape)
    score[...] = score_in[...] + alpha * query[...]


def last_kernel(
    mine, theirs, res_in, direc_in, rr_in, score_in, damp, low, query, pri_hi, pri_lo,
    stack_out, rr, score, known, out, own_image, res, direc, stack, perm, image,
):
    alpha, fresh = step_body(
        (mine, theirs), damp[0:1, 0:1], rr_in[:, 0:1], res_in, direc_in, low, query, pri_hi, pri_lo,
        own_image, res, direc, stack, perm, image,
    )
    out[...] = jnp.broadcast_to(rowsum(own_part(direc) * own_image[...]), out.shape)
    stack_out[...] = stack[...]
    size = jnp.zeros((COLS, 1), F32)
    for cols in BLOCKS:
        size = size + rowsum(direc[:, cols] * direc[:, cols])
    known[...] = jnp.broadcast_to(damp[0:1, 0:1] * size, known.shape)
    rr[...] = jnp.broadcast_to(fresh, rr.shape)
    score[...] = score_in[...] + alpha * query[...]


def cg_call(kernel, operands, outs, extra):
    n = operands[-1].shape[1]
    scratch = ([pltpu.VMEM((COLS, OWN), F32)] if extra else []) + [pltpu.VMEM((COLS, n), F32)] * extra + [
        pltpu.VMEM((2 * COLS, n), BF16), pltpu.VMEM((COLS, n), F32), pltpu.VMEM((COLS, n), F32)
    ]
    return pl.pallas_call(
        kernel,
        out_shape=outs,
        in_specs=[VMEM] * len(operands),
        out_specs=(VMEM,) * len(outs),
        scratch_shapes=scratch,
        compiler_params=params(24),
        name=kernel.__name__[:-7],
    )(*operands)


def iota(shape, axis):
    return lax.broadcasted_iota(jnp.int32, shape, axis)


exact = functools.partial(lax.dot_general, precision=HIGHEST, preferred_element_type=F32)


def own_columns(y, core):
    return (iota((8, COLS), 1) == iota((8, COLS), 0) + 4 * (y * CORES + core)).astype(F32)


def query_kernel(stack, f_hi, f_lo, score, size, own):
    x, z, _, y, core = place()
    q = against_factors(stack, f_hi, f_lo)
    rollouts = q.shape[1]
    size[...] = jnp.broadcast_to(rowsum(q * q) * (1.0 / rollouts), size.shape)
    pick = own_columns(y, core)
    both = jnp.concatenate([exact(pick, q, NN), exact(pick, score[...], NN)], axis=0)
    row = iota((rollouts, rollouts), 0)
    side = lax.rem(core + row // 128, CORES)
    third, second, first, last = row // 32 % 4, row // 8 % 4, row // 2 % 4, row % 2
    even = 1 - side
    dx = even * second + side * third
    dz = even * first + side * second
    dy = even * third + side * first
    home = lax.rem(x + SIDE - dx, SIDE) * SIDE + lax.rem(z + SIDE - dz, SIDE)
    rank = home * 16 + side * 8 + lax.rem(y + SIDE - dy, SIDE) * 2 + last
    own[...] = exact(both, (rank == iota((rollouts, rollouts), 1)).astype(F32), NN)


def last_query(stack, f_hi, f_lo, score):
    return pl.pallas_call(
        query_kernel,
        out_shape=(pltpu.VMEM((COLS, 128), F32), pltpu.VMEM((16, 256), F32)),
        in_specs=[VMEM] * 4,
        out_specs=(VMEM,) * 2,
        compiler_params=params(16),
        cost_estimate=cost(6 * 256 * 256 * f_hi.shape[1], 4 * 256 * f_hi.shape[1]),
        name="last_query",
    )(stack, f_hi, f_lo, score)


def finish_kernel(ours, theirs, known, size, rr, own, out):
    _, _, _, y, core = place()
    curve = (ours[...] + theirs[...]) + known[...] + size[...]
    alpha = exact(own_columns(y, core), rr[...] / curve, NN)[:, 0:1]
    ordered = own[8:16, :] + alpha * own[0:8, :]
    for i in range(16):
        part = ordered[:, i // 8 * 128 : (i // 8 + 1) * 128]
        shift = (128 - i % 8 * 16) % 128
        out[i] = pltpu.roll(part, shift, 1) if shift else part


def finish(ours, theirs, known, size, rr, own):
    return pl.pallas_call(
        finish_kernel,
        out_shape=jax.ShapeDtypeStruct((16, 8, 128), F32),
        in_specs=[VMEM] * 6,
        out_specs=VMEM,
        name="finish",
    )(*in_vmem([ours, theirs, known, size, rr, own]))


def place_kernel(parts, out, rows):
    for i in range(16):
        rows[4 * i : 4 * i + 4, :] = parts[i, 0:4, :]
    pick = lax.broadcasted_iota(jnp.int32, (16, 128), 0) == lax.broadcasted_iota(jnp.int32, (16, 128), 1)
    out[...] = lax.dot_general(pick.astype(F32), rows[...], NT, precision=HIGHEST, preferred_element_type=F32)


def place_scores(parts):
    return pl.pallas_call(
        place_kernel,
        out_shape=jax.ShapeDtypeStruct((16, 64), F32),
        in_specs=[VMEM],
        out_specs=VMEM,
        scratch_shapes=[pltpu.VMEM((64, 128), F32)],
        name="place_scores",
    )(parts)


BOTH = ("dp", "tensor")


def over_stage(value, stage):
    return [value] + [lax.ppermute(value, BOTH, shifted(d, stage)) for d in (1, 2, 3)]


def to_other_core(value):
    return lax.ppermute(value, "tensor", other_core())


def over_y(value):
    return [value] + [lax.ppermute(value, "tensor", along_y(d)) for d in (1, 2, 3)]


def join_image(pieces):
    line = jnp.concatenate(pieces, axis=1)
    return line, to_other_core(line)


def per_device(
    activations, out_grads, lengths, bank_in, index_in, bank_out, index_out, prior_cov, val_grads
):
    _, _, _, _, core = place()
    prior = lax.all_gather(own_slab(prior_cov), "dp", axis=0, tiled=True)

    tokens = (index_in, index_out, activations, out_grads, bank_in.transpose(0, 2, 1), bank_out.transpose(0, 2, 1))
    theirs = project(*tokens, True)
    from_core = to_other_core(theirs)
    mine = project(*tokens, False)
    to_y = [mine[2 * d : 2 * d + 2] + from_core[2 * d : 2 * d + 2] for d in (1, 2, 3)]
    to_y, start_here = lax.optimization_barrier((to_y, val_grads.T.reshape(16, 4, BLK)))
    from_y = [lax.ppermute(v, "tensor", along_y(d)) for d, v in zip((1, 2, 3), to_y)]
    start_here = lax.all_to_all(start_here, "dp", 0, 0, tiled=True)
    lengths, start_here = lax.optimization_barrier((lengths, start_here))

    own = factor(lengths, [mine[0:2], from_core[0:2], *from_y]).reshape(2, 4096)
    part = jnp.concatenate(over_stage(own, 0), axis=0)
    start_there = to_other_core(start_here)
    start_pair = jnp.where(
        core == 0,
        jnp.concatenate([start_here, start_there], axis=1),
        jnp.concatenate([start_there, start_here], axis=1),
    )
    part, start_pair = lax.optimization_barrier((part, start_pair))
    start_pieces = over_y(start_pair)
    moved = over_stage(part, 1)
    moved, start_pieces = lax.optimization_barrier((moved, start_pieces))
    near = over_stage(jnp.concatenate(moved, axis=0), 2)
    start, stack = assemble_start(start_pieces, prior_cov.shape[1])
    near[1], stack = lax.optimization_barrier((near[1], stack))
    far = [to_other_core(piece) for piece in near]
    far, prior = lax.optimization_barrier((far, prior))
    pri_hi, pri_lo, out = prior_image(stack, prior)
    pieces = over_y(out)
    f_hi, f_lo, query, low, square = take_factors(near + far, stack)
    pieces, square = lax.optimization_barrier((pieces, square))
    sds = jax.ShapeDtypeStruct
    n = start.shape[1]
    vector, flat = sds((COLS, n), F32), sds((COLS, 128), F32)
    scores_shape, part_shape = sds((COLS, 256), F32), sds((COLS, OWN), F32)
    state_shapes = (vector, vector, sds((2 * COLS, n), BF16), flat, scores_shape)
    res, direc, stack, rr, score, damp, out = cg_call(
        first_kernel,
        (*join_image(pieces), start, low, query, square, pri_hi, pri_lo),
        (*state_shapes, sds((8, 128), F32), part_shape), 0,
    )
    for iteration in range(1, ITERS - 1):
        pieces = over_y(out)
        query, low = low_rank_step(stack, f_hi, f_lo)
        pieces, query, low = lax.optimization_barrier((pieces, query, low))
        operands = (*join_image(pieces), res, direc, rr, score, damp, low, query, pri_hi, pri_lo)
        if iteration + 2 < ITERS:
            res, direc, stack, rr, score, out = cg_call(step_kernel, operands, (*state_shapes, part_shape), 0)
        else:
            stack, rr, score, known, out = cg_call(
                last_kernel, operands,
                (
                    pltpu.VMEM((2 * COLS, n), BF16), pltpu.VMEM((COLS, 128), F32), pltpu.VMEM((COLS, 256), F32),
                    pltpu.VMEM((COLS, 128), F32), pltpu.VMEM((COLS, 128), F32),
                ),
                2,
            )
    pieces = over_y(out)
    size, own = last_query(stack, f_hi, f_lo, score)
    pieces, size = lax.optimization_barrier((pieces, size))
    ours = (pieces[0] + pieces[1]) + (pieces[2] + pieces[3])
    parts = finish(ours, to_other_core(ours), known, size, rr, own)
    return place_scores(lax.all_to_all(parts, "dp", 0, 0, tiled=True))


def solution(mesh):
    return jax.shard_map(
        per_device,
        mesh=mesh,
        in_specs=(
            P("dp", None, "tensor"),
            P("dp", None, "tensor"),
            P("dp"),
            P(),
            P("tensor"),
            P(),
            P("tensor"),
            P("dp", None),
            P("dp", "tensor"),
        ),
        out_specs=P("dp", "tensor"),
        check_vma=False,
    )
```

profile of v0, /device:TPU:0, one launch (start us, length us, event | category | flops | bytes accessed | tf_op | source)
XLA Modules:
  0.0 208.4 jit_solution(2129559636174613546)
XLA Ops:
  6.5 1.8 own_slab.1
  8.4 7.1 %project.3 = f32[8,256,128]{2,1,0:T(8,128)S(1)} custom-call(s32[14]{0:T(128)S(1)} %copy-done, s32[4]{0:T(128)S(1)} %copy-done.1, bf16[16,256,1792]{2,1,0:T(8,128)(2,1)} %act.3, bf16[16,256,512]{2,1,0:T(8,128)(2,1)} %grad.3, bf16[16,64,128]{2,1,0:T(8,128)(2,1)} %bitcast.3, bf16[16,64,128]{2,1,0:T(8,128)(2,1)} %bitcast.5), custom_call_target="tpu_custom_call" | custom-call | flops 2415919104 | bytes 9437184 | tf_op jit(solution)/shard_map/project/pallas_call | solution.py:133
  15.7 7.1 %project.2 = f32[8,256,128]{2,1,0:T(8,128)S(1)} custom-call(s32[14]{0:T(128)S(1)} %copy-done, s32[4]{0:T(128)S(1)} %copy-done.1, bf16[16,256,1792]{2,1,0:T(8,128)(2,1)} %act.3, bf16[16,256,512]{2,1,0:T(8,128)(2,1)} %grad.3, bf16[16,64,128]{2,1,0:T(8,128)(2,1)} %bitcast.4, bf16[16,64,128]{2,1,0:T(8,128)(2,1)} %bitcast.6), custom_call_target="tpu_custom_call" | custom-call | flops 2415919104 | bytes 9437184 | tf_op jit(solution)/shard_map/project/pallas_call | solution.py:133
  23.0 1.7 collective-permute-start.1
  24.7 2.9 %collective-permute-start.2 = (f32[2,256,128]{2,1,0:T(8,128)S(1)}, f32[2,256,128]{2,1,0:T(8,128)S(1)}, u32[]{:S(2)}, u32[]{:S(2)}) collective-permute-start(f32[2,256,128]{2,1,0:T(8,128)S(1)} %get-tuple-element.115), channel_id=1, source_target_pairs={{0,4},{1,5},{2,6},{3,7},{4,0},{5,1},{6,2},{7,3},{8,12},{9,13},{10,... | collective-permute-start | bytes 786440 | tf_op jit(solution)/shard_map/ppermute | solution.py:610
  28.9 15.3 %all_to_all.10 = f32[16,4,256]{2,1,0:T(4,128)S(1)} all-to-all(f32[16,4,256]{2,1,0:T(4,128)S(1)} %reshape.6), channel_id=1, replica_groups=mesh['dp'=16,'tensor'=8] {'dp'}, dimensions={0} | all-to-all | bytes 131072 | tf_op jit(solution)/shard_map/all_to_all | solution.py:611
  49.8 1.7 collective-permute-done.6
  51.6 2.7 %collective-permute-done.5 = f32[2,4096]{1,0:T(2,128)S(1)} collective-permute-done((f32[2,4096]{1,0:T(2,128)S(1)}, f32[2,4096]{1,0:T(2,128)S(1)}, u32[]{:S(2)}, u32[]{:S(2)}) %collective-permute-start.5) | collective-permute-done | bytes 32800 | tf_op jit(solution)/shard_map/ppermute | solution.py:582
  61.1 2.2 %collective-permute-done.10 = f32[8,4096]{1,0:T(8,128)S(1)} collective-permute-done((f32[8,4096]{1,0:T(8,128)S(1)}, f32[8,4096]{1,0:T(8,128)S(1)}, u32[]{:S(2)}, u32[]{:S(2)}) %collective-permute-start.10) | collective-permute-done | bytes 131104 | tf_op jit(solution)/shard_map/ppermute | solution.py:582
  63.9 1.9 collective-permute-done.9
  65.9 2.2 %collective-permute-done.8 = f32[8,4096]{1,0:T(8,128)S(1)} collective-permute-done((f32[8,4096]{1,0:T(8,128)S(1)}, f32[8,4096]{1,0:T(8,128)S(1)}, u32[]{:S(2)}, u32[]{:S(2)}) %collective-permute-start.8) | collective-permute-done | bytes 131104 | tf_op jit(solution)/shard_map/ppermute | solution.py:582
  69.6 3.2 %collective-permute-start.19 = (f32[32,4096]{1,0:T(8,128)S(1)}, f32[32,4096]{1,0:T(8,128)S(1)}, u32[]{:S(2)}, u32[]{:S(2)}) collective-permute-start(f32[32,4096]{1,0:T(8,128)S(1)} %constant_dynamic-update-slice_fusion.n0), channel_id=1, source_target_pairs={{0,6},{1,97},{2,0},{3,99},{4,2},{5,101},{6,4},{7,103},{8,14},{9,10... | collective-permute-start | bytes 1572872 | tf_op jit(solution)/shard_map/ppermute | solution.py:582
  74.2 11.5 %collective-permute-done.14.n1 = f32[32,4096]{1,0:T(8,128)S(1)} collective-permute-done((f32[32,4096]{1,0:T(8,128)S(1)}, f32[32,4096]{1,0:T(8,128)S(1)}, u32[]{:S(2)}, u32[]{:S(2)}) %collective-permute-start.14) | collective-permute-done | bytes 524320 | tf_op jit(solution)/shard_map/ppermute | solution.py:582
  85.6 3.6 %collective-permute-start.20 = (f32[32,4096]{1,0:T(8,128)S(1)}, f32[32,4096]{1,0:T(8,128)S(1)}, u32[]{:S(2)}, u32[]{:S(2)}) collective-permute-start(f32[32,4096]{1,0:T(8,128)S(1)} %collective-permute-done.19.n3), channel_id=1, source_target_pairs={{0,1},{1,0},{2,3},{3,2},{4,5},{5,4},{6,7},{7,6},{8,9},{9,8},{10,11... | collective-permute-start | bytes 1572872 | tf_op jit(solution)/shard_map/ppermute | solution.py:586
  89.2 7.2 %collective-permute-start.18 = (f32[32,4096]{1,0:T(8,128)S(1)}, f32[32,4096]{1,0:T(8,128)S(1)}, u32[]{:S(2)}, u32[]{:S(2)}) collective-permute-start(f32[32,4096]{1,0:T(8,128)S(1)} %collective-permute-done.17.n2), channel_id=1, source_target_pairs={{0,1},{1,0},{2,3},{3,2},{4,5},{5,4},{6,7},{7,6},{8,9},{9,8},{10,11... | collective-permute-start | bytes 1572872 | tf_op jit(solution)/shard_map/ppermute | solution.py:586
  96.5 2.2 %collective-permute-done.18.m2 = f32[32,4096]{1,0:T(8,128)S(1)} collective-permute-done((f32[32,4096]{1,0:T(8,128)S(1)}, f32[32,4096]{1,0:T(8,128)S(1)}, u32[]{:S(2)}, u32[]{:S(2)}) %collective-permute-start.18) | collective-permute-done | bytes 524320 | tf_op jit(solution)/shard_map/ppermute | solution.py:586
  99.5 6.3 %prior_image.1 = (bf16[512,4096]{1,0:T(8,128)(2,1)S(1)}, bf16[512,4096]{1,0:T(8,128)(2,1)S(1)}, f32[40,512]{1,0:T(8,128)S(1)}) custom-call(bf16[64,4096]{1,0:T(8,128)(2,1)S(1)} %get-tuple-element.129.stack, f32[512,4096]{1,0:T(8,128)} %all-gather.2.cloned.1.call-done.prior_hbm), custom_call_target="tpu_custom_call" | custom-call | flops 3221225472 | bytes 16777216 | tf_op jit(solution)/shard_map/prior_image/pallas_call | solution.py:288
  105.9 2.8 %collective-permute-start.23 = (f32[40,512]{1,0:T(8,128)S(1)}, f32[40,512]{1,0:T(8,128)S(1)}, u32[]{:S(2)}, u32[]{:S(2)}) collective-permute-start(f32[40,512]{1,0:T(8,128)S(1)} %get-tuple-element.138), channel_id=1, source_target_pairs={{0,6},{1,7},{2,0},{3,1},{4,2},{5,3},{6,4},{7,5},{8,14},{9,15},{10,... | collective-permute-start | bytes 245768 | tf_op jit(solution)/shard_map/ppermute | solution.py:590
  110.4 5.4 %take_factors.1 = (bf16[256,4096]{1,0:T(8,128)(2,1)S(1)}, bf16[256,4096]{1,0:T(8,128)(2,1)S(1)}, f32[32,256]{1,0:T(8,128)S(1)}, f32[32,4096]{1,0:T(8,128)S(1)}, f32[8,128]{1,0:T(8,128)S(1)}) custom-call(f32[32,4096]{1,0:T(8,128)} %copy-done.7, f32[32,4096]{1,0:T(8,128)} %copy-done.8, f32[32,4096]{1,0:T(8,128)} %copy-done.10, f32[32,4096]{1,0:T(8,128)} %copy-done.9, ...), custom_call_target="tpu_custom_call" | custom-call | flops 3221225472 | bytes 8388608 | tf_op jit(solution)/shard_map/take_factors/pallas_call | solution.py:333
  118.1 3.9 %first.1 = (f32[32,4096]{1,0:T(8,128)S(1)}, f32[32,4096]{1,0:T(8,128)S(1)}, bf16[64,4096]{1,0:T(8,128)(2,1)S(1)}, f32[32,128]{1,0:T(8,128)S(1)}, f32[32,256]{1,0...) custom-call(f32[40,2048]{1,0:T(8,128)S(1)} %constant_dynamic-update-slice_fusion.4.mine, ...), custom_call_target="tpu_custom_call" | custom-call | tf_op jit(solution)/shard_map/first/pallas_call | solution.py:486
  122.1 1.9 collective-permute-start.27
  125.5 3.0 %low_rank.4 = (f32[32,256]{1,0:T(8,128)S(1)}, f32[32,4096]{1,0:T(8,128)S(1)}) custom-call(bf16[64,4096]{1,0:T(8,128)(2,1)S(1)} %get-tuple-element.149.stack, bf16[256,4096]{1,0:T(8,128)(2,1)S(1)} %get-tuple-element.150.f_hi, bf16[256,4096]{1,0:T(8,128)(2,1)S(1)} %get-tuple-element.151.f_lo), custom_call_target="tpu_custom_call" | custom-call | flops 3221225472 | bytes 4194304 | tf_op jit(solution)/shard_map/low_rank/pallas_call | solution.py:351
  132.7 4.0 %step.3 = (f32[32,4096]{1,0:T(8,128)S(1)}, f32[32,4096]{1,0:T(8,128)S(1)}, bf16[64,4096]{1,0:T(8,128)(2,1)S(1)}, f32[32,128]{1,0:T(8,128)S(1)}, f32[32,256]{1,0:T(8,128)S(1)}, /*index=5*/f32[32,512]{1,0:T(8,128)S(1)}) custom-call(f32[32,2048]{1,0:T(8,128)S(1)} %constant_dynamic-update-slice_fusion.8.mine, f32[32,2048]{1,0:T(8,128)S(1)} %collective-permute-done.28.theirs, ...), custom_call_target="tpu_custom_call" | custom-call | tf_op jit(solution)/shard_map/step/pallas_call | solution.py:486
  139.4 3.0 %low_rank.5 = (f32[32,256]{1,0:T(8,128)S(1)}, f32[32,4096]{1,0:T(8,128)S(1)}) custom-call(bf16[64,4096]{1,0:T(8,128)(2,1)S(1)} %get-tuple-element.166.stack, bf16[256,4096]{1,0:T(8,128)(2,1)S(1)} %get-tuple-element.150.f_hi, bf16[256,4096]{1,0:T(8,128)(2,1)S(1)} %get-tuple-element.151.f_lo), custom_call_target="tpu_custom_call" | custom-call | flops 3221225472 | bytes 4194304 | tf_op jit(solution)/shard_map/low_rank/pallas_call | solution.py:351
  146.1 4.0 %step.4 = (f32[32,4096]{1,0:T(8,128)S(1)}, f32[32,4096]{1,0:T(8,128)S(1)}, bf16[64,4096]{1,0:T(8,128)(2,1)S(1)}, f32[32,128]{1,0:T(8,128)S(1)}, f32[32,256]{1,0:T(8,128)S(1)}, /*index=5*/f32[32,512]{1,0:T(8,128)S(1)}) custom-call(f32[32,2048]{1,0:T(8,128)S(1)} %constant_dynamic-update-slice_fusion.12.mine, f32[32,2048]{1,0:T(8,128)S(1)} %collective-permute-done.32.theirs, ...), custom_call_target="tpu_custom_call" | custom-call | tf_op jit(solution)/shard_map/step/pallas_call | solution.py:486
  153.2 3.0 %low_rank.6 = (f32[32,256]{1,0:T(8,128)S(1)}, f32[32,4096]{1,0:T(8,128)S(1)}) custom-call(bf16[64,4096]{1,0:T(8,128)(2,1)S(1)} %get-tuple-element.180.stack, bf16[256,4096]{1,0:T(8,128)(2,1)S(1)} %get-tuple-element.150.f_hi, bf16[256,4096]{1,0:T(8,128)(2,1)S(1)} %get-tuple-element.151.f_lo), custom_call_target="tpu_custom_call" | custom-call | flops 3221225472 | bytes 4194304 | tf_op jit(solution)/shard_map/low_rank/pallas_call | solution.py:351
  156.2 1.7 collective-permute-done.34
  160.0 4.0 %step.5 = (f32[32,4096]{1,0:T(8,128)S(1)}, f32[32,4096]{1,0:T(8,128)S(1)}, bf16[64,4096]{1,0:T(8,128)(2,1)S(1)}, f32[32,128]{1,0:T(8,128)S(1)}, f32[32,256]{1,0:T(8,128)S(1)}, /*index=5*/f32[32,512]{1,0:T(8,128)S(1)}) custom-call(f32[32,2048]{1,0:T(8,128)S(1)} %constant_dynamic-update-slice_fusion.16.mine, f32[32,2048]{1,0:T(8,128)S(1)} %collective-permute-done.36.theirs, ...), custom_call_target="tpu_custom_call" | custom-call | tf_op jit(solution)/shard_map/step/pallas_call | solution.py:486
  166.5 3.0 %low_rank.7 = (f32[32,256]{1,0:T(8,128)S(1)}, f32[32,4096]{1,0:T(8,128)S(1)}) custom-call(bf16[64,4096]{1,0:T(8,128)(2,1)S(1)} %get-tuple-element.194.stack, bf16[256,4096]{1,0:T(8,128)(2,1)S(1)} %get-tuple-element.150.f_hi, bf16[256,4096]{1,0:T(8,128)(2,1)S(1)} %get-tuple-element.151.f_lo), custom_call_target="tpu_custom_call" | custom-call | flops 3221225472 | bytes 4194304 | tf_op jit(solution)/shard_map/low_rank/pallas_call | solution.py:351
  173.2 4.3 %last.1 = (bf16[64,4096]{1,0:T(8,128)(2,1)S(1)}, f32[32,128]{1,0:T(8,128)S(1)}, f32[32,256]{1,0:T(8,128)S(1)}, f32[32,128]{1,0:T(8,128)S(1)}, f32[32,128]{1,0:T(8,128)S(1)}) custom-call(f32[32,2048]{1,0:T(8,128)S(1)} %constant_dynamic-update-slice_fusion.20.mine, f32[32,2048]{1,0:T(8,128)S(1)} %collective-permute-done.40.theirs, ...), custom_call_target="tpu_custom_call" | custom-call | tf_op jit(solution)/shard_map/last/pallas_call | solution.py:486
  180.6 2.0 last_query.1
  187.0 12.9 %all_to_all.11.parts = f32[16,8,128]{2,1,0:T(8,128)} all-to-all(f32[16,8,128]{2,1,0:T(8,128)} %finish.1), channel_id=1, replica_groups=mesh['dp'=16,'tensor'=8] {'dp'}, dimensions={0} | all-to-all | bytes 131072 | tf_op jit(solution)/shard_map/all_to_all | solution.py:666
  (140 shorter events, 55.0 us)
Async XLA Ops:
  6.5 93.0 %all-gather.2.cloned.1.call-start = ((), (), s32[]{:S(2)}) async-start(), calls=%async_computation.2 | async-start | bytes 8912896 | tf_op jit(solution)/shard_map/all_gather | solution.py:602
  15.6 7.3 %collective-permute-start = (f32[8,256,128]{2,1,0:T(8,128)S(1)}, f32[8,256,128]{2,1,0:T(8,128)S(1)}, u32[]{:S(2)}, u32[]{:S(2)}) collective-permute-start(f32[8,256,128]{2,1,0:T(8,128)S(1)} %project.3), channel_id=1, source_target_pairs={{0,1},{1,0},{2,3},{3,2},{4,5},{5,4},{6,7},{7,6},{8,9},{9,8},{10,11... | collective-permute-start | bytes 3145736 | tf_op jit(solution)/shard_map/ppermute | solution.py:586
  23.0 21.3 %collective-permute-start.1 = (f32[2,256,128]{2,1,0:T(8,128)S(1)}, f32[2,256,128]{2,1,0:T(8,128)S(1)}, u32[]{:S(2)}, u32[]{:S(2)}) collective-permute-start(f32[2,256,128]{2,1,0:T(8,128)S(1)} %get-tuple-element.114), channel_id=1, source_target_pairs={{0,2},{1,3},{2,4},{3,5},{4,6},{5,7},{6,0},{7,1},{8,10},{9,11},{10,... | collective-permute-start | bytes 786440 | tf_op jit(solution)/shard_map/ppermute | solution.py:610
  24.7 19.6 %collective-permute-start.2 = (f32[2,256,128]{2,1,0:T(8,128)S(1)}, f32[2,256,128]{2,1,0:T(8,128)S(1)}, u32[]{:S(2)}, u32[]{:S(2)}) collective-permute-start(f32[2,256,128]{2,1,0:T(8,128)S(1)} %get-tuple-element.115), channel_id=1, source_target_pairs={{0,4},{1,5},{2,6},{3,7},{4,0},{5,1},{6,2},{7,3},{8,12},{9,13},{10,... | collective-permute-start | bytes 786440 | tf_op jit(solution)/shard_map/ppermute | solution.py:610
  27.6 16.7 %collective-permute-start.3 = (f32[2,256,128]{2,1,0:T(8,128)S(1)}, f32[2,256,128]{2,1,0:T(8,128)S(1)}, u32[]{:S(2)}, u32[]{:S(2)}) collective-permute-start(f32[2,256,128]{2,1,0:T(8,128)S(1)} %get-tuple-element.116), channel_id=1, source_target_pairs={{0,6},{1,7},{2,0},{3,1},{4,2},{5,3},{6,4},{7,5},{8,14},{9,15},{10,... | collective-permute-start | bytes 786440 | tf_op jit(solution)/shard_map/ppermute | solution.py:610
  48.2 6.1 %collective-permute-start.5 = (f32[2,4096]{1,0:T(2,128)S(1)}, f32[2,4096]{1,0:T(2,128)S(1)}, u32[]{:S(2)}, u32[]{:S(2)}) collective-permute-start(f32[2,4096]{1,0:T(2,128)S(1)} %reshape.7), channel_id=1, source_target_pairs={{0,16},{1,5},{2,18},{3,7},{4,20},{5,1},{6,22},{7,3},{8,24},{9,13},... | collective-permute-start | bytes 98312 | tf_op jit(solution)/shard_map/ppermute | solution.py:582
  49.6 5.8 %collective-permute-start.4 = (f32[2,4096]{1,0:T(2,128)S(1)}, f32[2,4096]{1,0:T(2,128)S(1)}, u32[]{:S(2)}, u32[]{:S(2)}) collective-permute-start(f32[2,4096]{1,0:T(2,128)S(1)} %reshape.7), channel_id=1, source_target_pairs={{0,8},{1,3},{2,10},{3,5},{4,12},{5,7},{6,14},{7,1},{8,16},{9,11},{... | collective-permute-start | bytes 98312 | tf_op jit(solution)/shard_map/ppermute | solution.py:582
  55.5 7.8 %collective-permute-start.10 = (f32[8,4096]{1,0:T(8,128)S(1)}, f32[8,4096]{1,0:T(8,128)S(1)}, u32[]{:S(2)}, u32[]{:S(2)}) collective-permute-start(f32[8,4096]{1,0:T(8,128)S(1)} %pad_maximum_fusion), channel_id=1, source_target_pairs={{0,96},{1,25},{2,98},{3,27},{4,100},{5,29},{6,102},{7,31},{8,104},... | collective-permute-start | bytes 393224 | tf_op jit(solution)/shard_map/ppermute | solution.py:582
  56.6 9.3 %collective-permute-start.9 = (f32[8,4096]{1,0:T(8,128)S(1)}, f32[8,4096]{1,0:T(8,128)S(1)}, u32[]{:S(2)}, u32[]{:S(2)}) collective-permute-start(f32[8,4096]{1,0:T(8,128)S(1)} %pad_maximum_fusion), channel_id=1, source_target_pairs={{0,64},{1,17},{2,66},{3,19},{4,68},{5,21},{6,70},{7,23},{8,72},{9,... | collective-permute-start | bytes 393224 | tf_op jit(solution)/shard_map/ppermute | solution.py:582
  58.1 10.0 %collective-permute-start.8 = (f32[8,4096]{1,0:T(8,128)S(1)}, f32[8,4096]{1,0:T(8,128)S(1)}, u32[]{:S(2)}, u32[]{:S(2)}) collective-permute-start(f32[8,4096]{1,0:T(8,128)S(1)} %pad_maximum_fusion), channel_id=1, source_target_pairs={{0,32},{1,9},{2,34},{3,11},{4,36},{5,13},{6,38},{7,15},{8,40},{9,1... | collective-permute-start | bytes 393224 | tf_op jit(solution)/shard_map/ppermute | solution.py:582
  58.2 9.9 %collective-permute-start.13 = (f32[16,8,256]{2,1,0:T(8,128)S(1)}, f32[16,8,256]{2,1,0:T(8,128)S(1)}, u32[]{:S(2)}, u32[]{:S(2)}) collective-permute-start(f32[16,8,256]{2,1,0:T(8,128)S(1)} %maximum_select_fusion.b0), channel_id=1, source_target_pairs={{0,6},{1,7},{2,0},{3,1},{4,2},{5,3},{6,4},{7,5},{8,14},{9,15},{10,... | collective-permute-start | bytes 393224 | tf_op jit(solution)/shard_map/ppermute | solution.py:590
  59.5 8.6 %collective-permute-start.12 = (f32[16,8,256]{2,1,0:T(8,128)S(1)}, f32[16,8,256]{2,1,0:T(8,128)S(1)}, u32[]{:S(2)}, u32[]{:S(2)}) collective-permute-start(f32[16,8,256]{2,1,0:T(8,128)S(1)} %maximum_select_fusion.b0), channel_id=1, source_target_pairs={{0,4},{1,5},{2,6},{3,7},{4,0},{5,1},{6,2},{7,3},{8,12},{9,13},{10,... | collective-permute-start | bytes 393224 | tf_op jit(solution)/shard_map/ppermute | solution.py:590
  63.3 6.2 %collective-permute-start.11 = (f32[16,8,256]{2,1,0:T(8,128)S(1)}, f32[16,8,256]{2,1,0:T(8,128)S(1)}, u32[]{:S(2)}, u32[]{:S(2)}) collective-permute-start(f32[16,8,256]{2,1,0:T(8,128)S(1)} %maximum_select_fusion.b0), channel_id=1, source_target_pairs={{0,2},{1,3},{2,4},{3,5},{4,6},{5,7},{6,0},{7,1},{8,10},{9,11},{10,... | collective-permute-start | bytes 393224 | tf_op jit(solution)/shard_map/ppermute | solution.py:590
  69.6 16.1 %collective-permute-start.14 = (f32[32,4096]{1,0:T(8,128)S(1)}, f32[32,4096]{1,0:T(8,128)S(1)}, u32[]{:S(2)}, u32[]{:S(2)}) collective-permute-start(f32[32,4096]{1,0:T(8,128)S(1)} %constant_dynamic-update-slice_fusion.n0), channel_id=1, source_target_pairs={{0,2},{1,33},{2,4},{3,35},{4,6},{5,37},{6,0},{7,39},{8,10},{9,41},... | collective-permute-start | bytes 1572872 | tf_op jit(solution)/shard_map/ppermute | solution.py:582
  69.6 16.0 %collective-permute-start.19 = (f32[32,4096]{1,0:T(8,128)S(1)}, f32[32,4096]{1,0:T(8,128)S(1)}, u32[]{:S(2)}, u32[]{:S(2)}) collective-permute-start(f32[32,4096]{1,0:T(8,128)S(1)} %constant_dynamic-update-slice_fusion.n0), channel_id=1, source_target_pairs={{0,6},{1,97},{2,0},{3,99},{4,2},{5,101},{6,4},{7,103},{8,14},{9,10... | collective-permute-start | bytes 1572872 | tf_op jit(solution)/shard_map/ppermute | solution.py:582
  72.9 16.4 %collective-permute-start.17 = (f32[32,4096]{1,0:T(8,128)S(1)}, f32[32,4096]{1,0:T(8,128)S(1)}, u32[]{:S(2)}, u32[]{:S(2)}) collective-permute-start(f32[32,4096]{1,0:T(8,128)S(1)} %constant_dynamic-update-slice_fusion.n0), channel_id=1, source_target_pairs={{0,4},{1,65},{2,6},{3,67},{4,0},{5,69},{6,2},{7,71},{8,12},{9,73},... | collective-permute-start | bytes 1572872 | tf_op jit(solution)/shard_map/ppermute | solution.py:582
  72.9 23.6 %collective-permute-start.15 = (f32[32,4096]{1,0:T(8,128)S(1)}, f32[32,4096]{1,0:T(8,128)S(1)}, u32[]{:S(2)}, u32[]{:S(2)}) collective-permute-start(f32[32,4096]{1,0:T(8,128)S(1)} %constant_dynamic-update-slice_fusion.n0), channel_id=1, source_target_pairs={{0,1},{1,0},{2,3},{3,2},{4,5},{5,4},{6,7},{7,6},{8,9},{9,8},{10,11... | collective-permute-start | bytes 1572872 | tf_op jit(solution)/shard_map/ppermute | solution.py:586
  85.6 10.8 %collective-permute-start.20 = (f32[32,4096]{1,0:T(8,128)S(1)}, f32[32,4096]{1,0:T(8,128)S(1)}, u32[]{:S(2)}, u32[]{:S(2)}) collective-permute-start(f32[32,4096]{1,0:T(8,128)S(1)} %collective-permute-done.19.n3), channel_id=1, source_target_pairs={{0,1},{1,0},{2,3},{3,2},{4,5},{5,4},{6,7},{7,6},{8,9},{9,8},{10,11... | collective-permute-start | bytes 1572872 | tf_op jit(solution)/shard_map/ppermute | solution.py:586
  89.2 9.5 %collective-permute-start.18 = (f32[32,4096]{1,0:T(8,128)S(1)}, f32[32,4096]{1,0:T(8,128)S(1)}, u32[]{:S(2)}, u32[]{:S(2)}) collective-permute-start(f32[32,4096]{1,0:T(8,128)S(1)} %collective-permute-done.17.n2), channel_id=1, source_target_pairs={{0,1},{1,0},{2,3},{3,2},{4,5},{5,4},{6,7},{7,6},{8,9},{9,8},{10,11... | collective-permute-start | bytes 1572872 | tf_op jit(solution)/shard_map/ppermute | solution.py:586
  105.9 9.9 %collective-permute-start.23 = (f32[40,512]{1,0:T(8,128)S(1)}, f32[40,512]{1,0:T(8,128)S(1)}, u32[]{:S(2)}, u32[]{:S(2)}) collective-permute-start(f32[40,512]{1,0:T(8,128)S(1)} %get-tuple-element.138), channel_id=1, source_target_pairs={{0,6},{1,7},{2,0},{3,1},{4,2},{5,3},{6,4},{7,5},{8,14},{9,15},{10,... | collective-permute-start | bytes 245768 | tf_op jit(solution)/shard_map/ppermute | solution.py:590
  108.7 7.1 %collective-permute-start.22 = (f32[40,512]{1,0:T(8,128)S(1)}, f32[40,512]{1,0:T(8,128)S(1)}, u32[]{:S(2)}, u32[]{:S(2)}) collective-permute-start(f32[40,512]{1,0:T(8,128)S(1)} %get-tuple-element.138), channel_id=1, source_target_pairs={{0,4},{1,5},{2,6},{3,7},{4,0},{5,1},{6,2},{7,3},{8,12},{9,13},{10,... | collective-permute-start | bytes 245768 | tf_op jit(solution)/shard_map/ppermute | solution.py:590
  109.5 6.9 %collective-permute-start.21 = (f32[40,512]{1,0:T(8,128)S(1)}, f32[40,512]{1,0:T(8,128)S(1)}, u32[]{:S(2)}, u32[]{:S(2)}) collective-permute-start(f32[40,512]{1,0:T(8,128)S(1)} %get-tuple-element.138), channel_id=1, source_target_pairs={{0,2},{1,3},{2,4},{3,5},{4,6},{5,7},{6,0},{7,1},{8,10},{9,11},{10,... | collective-permute-start | bytes 245768 | tf_op jit(solution)/shard_map/ppermute | solution.py:590
  122.1 6.4 %collective-permute-start.27 = (f32[32,512]{1,0:T(8,128)S(1)}, f32[32,512]{1,0:T(8,128)S(1)}, u32[]{:S(2)}, u32[]{:S(2)}) collective-permute-start(f32[32,512]{1,0:T(8,128)S(1)} %get-tuple-element.154), channel_id=1, source_target_pairs={{0,6},{1,7},{2,0},{3,1},{4,2},{5,3},{6,4},{7,5},{8,14},{9,15},{10,... | collective-permute-start | bytes 196616 | tf_op jit(solution)/shard_map/ppermute | solution.py:590
  124.0 6.2 %collective-permute-start.26 = (f32[32,512]{1,0:T(8,128)S(1)}, f32[32,512]{1,0:T(8,128)S(1)}, u32[]{:S(2)}, u32[]{:S(2)}) collective-permute-start(f32[32,512]{1,0:T(8,128)S(1)} %get-tuple-element.154), channel_id=1, source_target_pairs={{0,4},{1,5},{2,6},{3,7},{4,0},{5,1},{6,2},{7,3},{8,12},{9,13},{10,... | collective-permute-start | bytes 196616 | tf_op jit(solution)/shard_map/ppermute | solution.py:590
  136.6 5.7 %collective-permute-start.31 = (f32[32,512]{1,0:T(8,128)S(1)}, f32[32,512]{1,0:T(8,128)S(1)}, u32[]{:S(2)}, u32[]{:S(2)}) collective-permute-start(f32[32,512]{1,0:T(8,128)S(1)} %get-tuple-element.169), channel_id=1, source_target_pairs={{0,6},{1,7},{2,0},{3,1},{4,2},{5,3},{6,4},{7,5},{8,14},{9,15},{10,... | collective-permute-start | bytes 196616 | tf_op jit(solution)/shard_map/ppermute | solution.py:590
  137.5 6.1 %collective-permute-start.30 = (f32[32,512]{1,0:T(8,128)S(1)}, f32[32,512]{1,0:T(8,128)S(1)}, u32[]{:S(2)}, u32[]{:S(2)}) collective-permute-start(f32[32,512]{1,0:T(8,128)S(1)} %get-tuple-element.169), channel_id=1, source_target_pairs={{0,4},{1,5},{2,6},{3,7},{4,0},{5,1},{6,2},{7,3},{8,12},{9,13},{10,... | collective-permute-start | bytes 196616 | tf_op jit(solution)/shard_map/ppermute | solution.py:590
  138.5 5.7 %collective-permute-start.29 = (f32[32,512]{1,0:T(8,128)S(1)}, f32[32,512]{1,0:T(8,128)S(1)}, u32[]{:S(2)}, u32[]{:S(2)}) collective-permute-start(f32[32,512]{1,0:T(8,128)S(1)} %get-tuple-element.169), channel_id=1, source_target_pairs={{0,2},{1,3},{2,4},{3,5},{4,6},{5,7},{6,0},{7,1},{8,10},{9,11},{10,... | collective-permute-start | bytes 196616 | tf_op jit(solution)/shard_map/ppermute | solution.py:590
  150.1 6.1 %collective-permute-start.35 = (f32[32,512]{1,0:T(8,128)S(1)}, f32[32,512]{1,0:T(8,128)S(1)}, u32[]{:S(2)}, u32[]{:S(2)}) collective-permute-start(f32[32,512]{1,0:T(8,128)S(1)} %get-tuple-element.183), channel_id=1, source_target_pairs={{0,6},{1,7},{2,0},{3,1},{4,2},{5,3},{6,4},{7,5},{8,14},{9,15},{10,... | collective-permute-start | bytes 196616 | tf_op jit(solution)/shard_map/ppermute | solution.py:590
  151.6 6.3 %collective-permute-start.34 = (f32[32,512]{1,0:T(8,128)S(1)}, f32[32,512]{1,0:T(8,128)S(1)}, u32[]{:S(2)}, u32[]{:S(2)}) collective-permute-start(f32[32,512]{1,0:T(8,128)S(1)} %get-tuple-element.183), channel_id=1, source_target_pairs={{0,4},{1,5},{2,6},{3,7},{4,0},{5,1},{6,2},{7,3},{8,12},{9,13},{10,... | collective-permute-start | bytes 196616 | tf_op jit(solution)/shard_map/ppermute | solution.py:590
  152.5 5.9 %collective-permute-start.33 = (f32[32,512]{1,0:T(8,128)S(1)}, f32[32,512]{1,0:T(8,128)S(1)}, u32[]{:S(2)}, u32[]{:S(2)}) collective-permute-start(f32[32,512]{1,0:T(8,128)S(1)} %get-tuple-element.183), channel_id=1, source_target_pairs={{0,2},{1,3},{2,4},{3,5},{4,6},{5,7},{6,0},{7,1},{8,10},{9,11},{10,... | collective-permute-start | bytes 196616 | tf_op jit(solution)/shard_map/ppermute | solution.py:590
  164.8 6.1 %collective-permute-start.38 = (f32[32,512]{1,0:T(8,128)S(1)}, f32[32,512]{1,0:T(8,128)S(1)}, u32[]{:S(2)}, u32[]{:S(2)}) collective-permute-start(f32[32,512]{1,0:T(8,128)S(1)} %get-tuple-element.197), channel_id=1, source_target_pairs={{0,4},{1,5},{2,6},{3,7},{4,0},{5,1},{6,2},{7,3},{8,12},{9,13},{10,... | collective-permute-start | bytes 196616 | tf_op jit(solution)/shard_map/ppermute | solution.py:590
  165.9 5.7 %collective-permute-start.37 = (f32[32,512]{1,0:T(8,128)S(1)}, f32[32,512]{1,0:T(8,128)S(1)}, u32[]{:S(2)}, u32[]{:S(2)}) collective-permute-start(f32[32,512]{1,0:T(8,128)S(1)} %get-tuple-element.197), channel_id=1, source_target_pairs={{0,2},{1,3},{2,4},{3,5},{4,6},{5,7},{6,0},{7,1},{8,10},{9,11},{10,... | collective-permute-start | bytes 196616 | tf_op jit(solution)/shard_map/ppermute | solution.py:590
  (28 other events, 194.8 us)
Sparse Core Ops, SparseCore 0:
  9.5 82.9 all-gather.1
where the time goes:
time: 209 us; the launch traced here: 208 us
  Pallas kernels  67.2 us (32%)
  starting transfers between devices  49.5 us (24%)
  waiting for transfers between devices  47.3 us (23%)
  blocking collectives  28.2 us (13%)
  between operations  14 us (7%)
    ppermute x9, waiting for transfers between devices, over_stage(): lax.ppermute(value, BOTH, shifted(d, stage))  23.3 us
    ppermute x21, starting transfers between devices, over_y(): lax.ppermute(value, 'tensor', along_y(d))  23 us
    pallas_call x5, Pallas kernels, cg_call(): pl.pallas_call(kernel, out_shape=outs, in_specs=[VMEM] * len(operands), o...  20.1 us
    all_to_all x1, blocking collectives, per_device(): start_here = lax.all_to_all(start_here, 'dp', 0, 0, tiled=True)  15.3 us
    pallas_call x2, Pallas kernels, project(): pl.pallas_call(functools.partial(project_kernel, flip=flip), out_shape=ja...  14.2 us
    all_to_all x1, blocking collectives, per_device(): return place_scores(lax.all_to_all(parts, 'dp', 0, 0, tiled=True))  12.9 us
    ppermute x21, waiting for transfers between devices, over_y(): lax.ppermute(value, 'tensor', along_y(d))  12.8 us
    pallas_call x4, Pallas kernels, low_rank_step(): pl.pallas_call(low_rank, out_shape=(sds((COLS, 256), F32), sds((COLS, n),...  11.9 us
  transfers between devices with their start and end apart: 46, of which 26 were waited for; matrix products, arithmetic and copies ran while one was open for 1% of the time, Pallas kernels for 17%

commit v1 on v0

--- a/solution.py
+++ b/solution.py
@@ -181,13 +181,15 @@
         total = (v0[r] + v1[r]) + (w1[r] + w2[r]) + w3[r]
         used = lax.broadcasted_iota(jnp.int32, (slots, 64), 0) < lens[core * 8 + y * 2 + r]
         grad = jnp.where(used, total[:, 64:128], 0.0)
-        out[r] = mm3(split(grad), split(total[:, 0:64]), TN)
+        product = mm3(split(grad), split(total[:, 0:64]), TN)
+        for k in range(64):
+            out[r : r + 1, k * 64 : (k + 1) * 64] = product[k : k + 1, :]
 
 
 def factor(lens, pieces):
     return pl.pallas_call(
         factor_kernel,
-        out_shape=jax.ShapeDtypeStruct((2, 64, 64), F32),
+        out_shape=jax.ShapeDtypeStruct((2, 4096), F32),
         in_specs=[SMEM] + [VMEM] * 5,
         out_specs=VMEM,
         name="factor",
@@ -606,26 +608,26 @@
     from_core = to_other_core(theirs)
     mine = project(*tokens, False)
     to_y = [mine[2 * d : 2 * d + 2] + from_core[2 * d : 2 * d + 2] for d in (1, 2, 3)]
-    to_y, start_here = lax.optimization_barrier((to_y, val_grads.T.reshape(16, 4, BLK)))
     from_y = [lax.ppermute(v, "tensor", along_y(d)) for d, v in zip((1, 2, 3), to_y)]
+    own = factor(lengths, [mine[0:2], from_core[0:2], *from_y])
+    part = jnp.concatenate(over_stage(own, 0), axis=0)
+    part, start_here = lax.optimization_barrier((part, val_grads.T.reshape(16, 4, BLK)))
+    moved = over_stage(part, 1)
     start_here = lax.all_to_all(start_here, "dp", 0, 0, tiled=True)
-    lengths, start_here = lax.optimization_barrier((lengths, start_here))
-
-    own = factor(lengths, [mine[0:2], from_core[0:2], *from_y]).reshape(2, 4096)
-    part = jnp.concatenate(over_stage(own, 0), axis=0)
+    moved, start_here = lax.optimization_barrier((moved, start_here))
+    near = over_stage(jnp.concatenate(moved, axis=0), 2)
     start_there = to_other_core(start_here)
     start_pair = jnp.where(
         core == 0,
         jnp.concatenate([start_here, start_there], axis=1),
         jnp.concatenate([start_there, start_here], axis=1),
     )
-    part, start_pair = lax.optimization_barrier((part, start_pair))
     start_pieces = over_y(start_pair)
-    moved = over_stage(part, 1)
-    moved, start_pieces = lax.optimization_barrier((moved, start_pieces))
-    near = over_stage(jnp.concatenate(moved, axis=0), 2)
+    near[0], start_pieces = lax.optimization_barrier((near[0], start_pieces))
+    near[3], start_pieces = lax.optimization_barrier((near[3], start_pieces))
     start, stack = assemble_start(start_pieces, prior_cov.shape[1])
     near[1], stack = lax.optimization_barrier((near[1], stack))
+    near[2], stack = lax.optimization_barrier((near[2], stack))
     far = [to_other_core(piece) for piece in near]
     far, prior = lax.optimization_barrier((far, prior))
     pri_hi, pri_lo, out = prior_image(stack, prior)

time: 209 us -> 210 us (level)
  waiting for transfers between devices: 47.3 us -> 57.9 us
  starting transfers between devices: 49.5 us -> 42.2 us
  blocking collectives: 28.2 us -> 25.9 us
    ppermute x9, waiting for transfers between devices: 23.3 us -> 5.09 us  [over_stage(): lax.ppermute(value, BOTH, shifted(d, stage))]
    ppermute x21, waiting for transfers between devices: 12.8 us -> 27.3 us  [over_y(): lax.ppermute(value, 'tensor', along_y(d))]
    ppermute x3, waiting for transfers between devices: 0.01 us -> 13.9 us  [per_device(): lax.ppermute(v, 'tensor', along_y(d))]
    ppermute x12, starting transfers between devices: 11.6 us -> 1.91 us  [to_other_core(): return lax.ppermute(value, 'tensor', other_core())]
    ppermute x9, starting transfers between devices: 8.87 us -> 12.3 us  [over_stage(): lax.ppermute(value, BOTH, shifted(d, stage))]
  transfers between devices with their start and end apart: 46 -> 46, of which waited for: 26 -> 28; matrix products, arithmetic and copies ran while one was open for 1% -> 1% of each run, Pallas kernels for 17% -> 17%
where the time goes in v1:
time: 210 us; the launch traced here: 209 us
  Pallas kernels  67.2 us (32%)
  waiting for transfers between devices  57.9 us (28%)
  starting transfers between devices  42.2 us (20%)
  blocking collectives  25.9 us (12%)
  between operations  13.9 us (7%)
    ppermute x21, waiting for transfers between devices, over_y(): lax.ppermute(value, 'tensor', along_y(d))  27.3 us
    ppermute x21, starting transfers between devices, over_y(): lax.ppermute(value, 'tensor', along_y(d))  23.2 us
    pallas_call x5, Pallas kernels, cg_call(): pl.pallas_call(kernel, out_shape=outs, in_specs=[VMEM] * len(operands), o...  20.1 us
    pallas_call x2, Pallas kernels, project(): pl.pallas_call(functools.partial(project_kernel, flip=flip), out_shape=ja...  14.2 us
    all_to_all x1, blocking collectives, per_device(): start_here = lax.all_to_all(start_here, 'dp', 0, 0, tiled=True)  14.1 us
    ppermute x3, waiting for transfers between devices, per_device(): lax.ppermute(v, 'tensor', along_y(d))  13.9 us
    ppermute x9, starting transfers between devices, over_stage(): lax.ppermute(value, BOTH, shifted(d, stage))  12.3 us
    pallas_call x4, Pallas kernels, low_rank_step(): pl.pallas_call(low_rank, out_shape=(sds((COLS, 256), F32), sds((COLS, n),...  11.9 us
  transfers between devices with their start and end apart: 46, of which 28 were waited for; matrix products, arithmetic and copies ran while one was open for 1% of the time, Pallas kernels for 17%

profile of v1, /device:TPU:0, one launch (start us, length us, event | category | flops | bytes accessed | tf_op | source)
XLA Modules:
  0.0 209.2 jit_solution(11852178337599402637)
XLA Ops:
  6.5 1.8 own_slab.1
  8.4 7.1 %project.3 = f32[8,256,128]{2,1,0:T(8,128)S(1)} custom-call(s32[14]{0:T(128)S(1)} %copy-done, s32[4]{0:T(128)S(1)} %copy-done.1, bf16[16,256,1792]{2,1,0:T(8,128)(2,1)} %act.3, bf16[16,256,512]{2,1,0:T(8,128)(2,1)} %grad.3, bf16[16,64,128]{2,1,0:T(8,128)(2,1)} %bitcast.3, bf16[16,64,128]{2,1,0:T(8,128)(2,1)} %bitcast.5), custom_call_target="tpu_custom_call" | custom-call | flops 2415919104 | bytes 9437184 | tf_op jit(solution)/shard_map/project/pallas_call | solution.py:133
  15.6 7.1 %project.2 = f32[8,256,128]{2,1,0:T(8,128)S(1)} custom-call(s32[14]{0:T(128)S(1)} %copy-done, s32[4]{0:T(128)S(1)} %copy-done.1, bf16[16,256,1792]{2,1,0:T(8,128)(2,1)} %act.3, bf16[16,256,512]{2,1,0:T(8,128)(2,1)} %grad.3, bf16[16,64,128]{2,1,0:T(8,128)(2,1)} %bitcast.4, bf16[16,64,128]{2,1,0:T(8,128)(2,1)} %bitcast.6), custom_call_target="tpu_custom_call" | custom-call | flops 2415919104 | bytes 9437184 | tf_op jit(solution)/shard_map/project/pallas_call | solution.py:133
  22.9 3.2 %collective-permute-start.3 = (f32[2,256,128]{2,1,0:T(8,128)S(1)}, f32[2,256,128]{2,1,0:T(8,128)S(1)}, u32[]{:S(2)}, u32[]{:S(2)}) collective-permute-start(f32[2,256,128]{2,1,0:T(8,128)S(1)} %get-tuple-element.225), channel_id=1, source_target_pairs={{0,6},{1,7},{2,0},{3,1},{4,2},{5,3},{6,4},{7,5},{8,14},{9,15},{10,... | collective-permute-start | bytes 786440 | tf_op jit(solution)/shard_map/ppermute | solution.py:611
  27.7 10.2 %collective-permute-done.3.w3 = f32[2,256,128]{2,1,0:T(8,128)S(1)} collective-permute-done((f32[2,256,128]{2,1,0:T(8,128)S(1)}, f32[2,256,128]{2,1,0:T(8,128)S(1)}, u32[]{:S(2)}, u32[]{:S(2)}) %collective-permute-start.3) | collective-permute-done | bytes 262176 | tf_op jit(solution)/shard_map/ppermute | solution.py:611
  37.9 3.7 %collective-permute-done.1.w1 = f32[2,256,128]{2,1,0:T(8,128)S(1)} collective-permute-done((f32[2,256,128]{2,1,0:T(8,128)S(1)}, f32[2,256,128]{2,1,0:T(8,128)S(1)}, u32[]{:S(2)}, u32[]{:S(2)}) %collective-permute-start.1) | collective-permute-done | bytes 262176 | tf_op jit(solution)/shard_map/ppermute | solution.py:611
  41.6 1.7 factor.1
  43.4 4.0 %collective-permute-start.6 = (f32[2,4096]{1,0:T(2,128)}, f32[2,4096]{1,0:T(2,128)S(1)}, u32[]{:S(2)}, u32[]{:S(2)}) collective-permute-start(f32[2,4096]{1,0:T(2,128)} %factor.1), channel_id=1, source_target_pairs={{0,24},{1,7},{2,26},{3,1},{4,28},{5,3},{6,30},{7,5},{8,0},{9,15},{... | collective-permute-start | bytes 98312 | tf_op jit(solution)/shard_map/ppermute | solution.py:584
  49.7 4.0 %collective-permute-done.5 = f32[2,4096]{1,0:T(2,128)S(1)} collective-permute-done((f32[2,4096]{1,0:T(2,128)}, f32[2,4096]{1,0:T(2,128)S(1)}, u32[]{:S(2)}, u32[]{:S(2)}) %collective-permute-start.5) | collective-permute-done | bytes 32800 | tf_op jit(solution)/shard_map/ppermute | solution.py:584
  54.6 2.8 %collective-permute-start.9 = (f32[8,4096]{1,0:T(8,128)S(1)}, f32[8,4096]{1,0:T(8,128)S(1)}, u32[]{:S(2)}, u32[]{:S(2)}) collective-permute-start(f32[8,4096]{1,0:T(8,128)S(1)} %pad_maximum_fusion), channel_id=1, source_target_pairs={{0,96},{1,25},{2,98},{3,27},{4,100},{5,29},{6,102},{7,31},{8,104},... | collective-permute-start | bytes 393224 | tf_op jit(solution)/shard_map/ppermute | solution.py:584
  59.1 14.1 %all_to_all.10 = f32[16,4,256]{2,1,0:T(4,128)S(1)} all-to-all(f32[16,4,256]{2,1,0:T(4,128)S(1)} %reshape.3), channel_id=1, replica_groups=mesh['dp'=16,'tensor'=8] {'dp'}, dimensions={0} | all-to-all | bytes 131072 | tf_op jit(solution)/shard_map/all_to_all | solution.py:616
  73.7 1.6 collective-permute-start.11
  77.1 2.3 %collective-permute-start.16 = (f32[16,8,256]{2,1,0:T(8,128)S(1)}, f32[16,8,256]{2,1,0:T(8,128)S(1)}, u32[]{:S(2)}, u32[]{:S(2)}) collective-permute-start(f32[16,8,256]{2,1,0:T(8,128)S(1)} %maximum_select_fusion.b0), channel_id=1, source_target_pairs={{0,6},{1,7},{2,0},{3,1},{4,2},{5,3},{6,4},{7,5},{8,14},{9,15},{10,... | collective-permute-start | bytes 393224 | tf_op jit(solution)/shard_map/ppermute | solution.py:592
  79.4 1.8 collective-permute-start.15
  81.3 11.1 %collective-permute-done.16.b3 = f32[16,8,256]{2,1,0:T(8,128)S(1)} collective-permute-done((f32[16,8,256]{2,1,0:T(8,128)S(1)}, f32[16,8,256]{2,1,0:T(8,128)S(1)}, u32[]{:S(2)}, u32[]{:S(2)}) %collective-permute-start.16) | collective-permute-done | bytes 131104 | tf_op jit(solution)/shard_map/ppermute | solution.py:592
  92.4 6.2 %collective-permute-done.14.b1 = f32[16,8,256]{2,1,0:T(8,128)S(1)} collective-permute-done((f32[16,8,256]{2,1,0:T(8,128)S(1)}, f32[16,8,256]{2,1,0:T(8,128)S(1)}, u32[]{:S(2)}, u32[]{:S(2)}) %collective-permute-start.14) | collective-permute-done | bytes 131104 | tf_op jit(solution)/shard_map/ppermute | solution.py:592
  103.3 6.3 %prior_image.1 = (bf16[512,4096]{1,0:T(8,128)(2,1)S(1)}, bf16[512,4096]{1,0:T(8,128)(2,1)S(1)}, f32[40,512]{1,0:T(8,128)S(1)}) custom-call(bf16[64,4096]{1,0:T(8,128)(2,1)S(1)} %get-tuple-element.132.stack, f32[512,4096]{1,0:T(8,128)} %all-gather.2.cloned.1.call-done.prior_hbm), custom_call_target="tpu_custom_call" | custom-call | flops 3221225472 | bytes 16777216 | tf_op jit(solution)/shard_map/prior_image/pallas_call | solution.py:290
  111.8 5.4 %take_factors.1 = (bf16[256,4096]{1,0:T(8,128)(2,1)S(1)}, bf16[256,4096]{1,0:T(8,128)(2,1)S(1)}, f32[32,256]{1,0:T(8,128)S(1)}, f32[32,4096]{1,0:T(8,128)S(1)}, f32[8,128]{1,0:T(8,128)S(1)}) custom-call(f32[32,4096]{1,0:T(8,128)} %copy-done.7, f32[32,4096]{1,0:T(8,128)} %copy-done.9, f32[32,4096]{1,0:T(8,128)} %copy-done.10, f32[32,4096]{1,0:T(8,128)} %copy-done.8, ...), custom_call_target="tpu_custom_call" | custom-call | flops 3221225472 | bytes 8388608 | tf_op jit(solution)/shard_map/take_factors/pallas_call | solution.py:335
  117.7 1.6 collective-permute-done.24.theirs
  119.4 4.0 %first.1 = (f32[32,4096]{1,0:T(8,128)S(1)}, f32[32,4096]{1,0:T(8,128)S(1)}, bf16[64,4096]{1,0:T(8,128)(2,1)S(1)}, f32[32,128]{1,0:T(8,128)S(1)}, f32[32,256]{1,0...) custom-call(f32[40,2048]{1,0:T(8,128)S(1)} %constant_dynamic-update-slice_fusion.4.mine, ...), custom_call_target="tpu_custom_call" | custom-call | tf_op jit(solution)/shard_map/first/pallas_call | solution.py:488
  123.3 2.4 %collective-permute-start.27 = (f32[32,512]{1,0:T(8,128)S(1)}, f32[32,512]{1,0:T(8,128)S(1)}, u32[]{:S(2)}, u32[]{:S(2)}) collective-permute-start(f32[32,512]{1,0:T(8,128)S(1)} %get-tuple-element.160), channel_id=1, source_target_pairs={{0,6},{1,7},{2,0},{3,1},{4,2},{5,3},{6,4},{7,5},{8,14},{9,15},{10,... | collective-permute-start | bytes 196616 | tf_op jit(solution)/shard_map/ppermute | solution.py:592
  128.6 3.0 %low_rank.4 = (f32[32,256]{1,0:T(8,128)S(1)}, f32[32,4096]{1,0:T(8,128)S(1)}) custom-call(bf16[64,4096]{1,0:T(8,128)(2,1)S(1)} %get-tuple-element.155.stack, bf16[256,4096]{1,0:T(8,128)(2,1)S(1)} %get-tuple-element.156.f_hi, bf16[256,4096]{1,0:T(8,128)(2,1)S(1)} %get-tuple-element.157.f_lo), custom_call_target="tpu_custom_call" | custom-call | flops 3221225472 | bytes 4194304 | tf_op jit(solution)/shard_map/low_rank/pallas_call | solution.py:353
  134.6 4.0 %step.3 = (f32[32,4096]{1,0:T(8,128)S(1)}, f32[32,4096]{1,0:T(8,128)S(1)}, bf16[64,4096]{1,0:T(8,128)(2,1)S(1)}, f32[32,128]{1,0:T(8,128)S(1)}, f32[32,256]{1,0:T(8,128)S(1)}, /*index=5*/f32[32,512]{1,0:T(8,128)S(1)}) custom-call(f32[32,2048]{1,0:T(8,128)S(1)} %constant_dynamic-update-slice_fusion.8.mine, f32[32,2048]{1,0:T(8,128)S(1)} %collective-permute-done.28.theirs, ...), custom_call_target="tpu_custom_call" | custom-call | tf_op jit(solution)/shard_map/step/pallas_call | solution.py:488
  141.3 3.0 %low_rank.5 = (f32[32,256]{1,0:T(8,128)S(1)}, f32[32,4096]{1,0:T(8,128)S(1)}) custom-call(bf16[64,4096]{1,0:T(8,128)(2,1)S(1)} %get-tuple-element.172.stack, bf16[256,4096]{1,0:T(8,128)(2,1)S(1)} %get-tuple-element.156.f_hi, bf16[256,4096]{1,0:T(8,128)(2,1)S(1)} %get-tuple-element.157.f_lo), custom_call_target="tpu_custom_call" | custom-call | flops 3221225472 | bytes 4194304 | tf_op jit(solution)/shard_map/low_rank/pallas_call | solution.py:353
  148.0 4.0 %step.4 = (f32[32,4096]{1,0:T(8,128)S(1)}, f32[32,4096]{1,0:T(8,128)S(1)}, bf16[64,4096]{1,0:T(8,128)(2,1)S(1)}, f32[32,128]{1,0:T(8,128)S(1)}, f32[32,256]{1,0:T(8,128)S(1)}, /*index=5*/f32[32,512]{1,0:T(8,128)S(1)}) custom-call(f32[32,2048]{1,0:T(8,128)S(1)} %constant_dynamic-update-slice_fusion.12.mine, f32[32,2048]{1,0:T(8,128)S(1)} %collective-permute-done.32.theirs, ...), custom_call_target="tpu_custom_call" | custom-call | tf_op jit(solution)/shard_map/step/pallas_call | solution.py:488
  155.2 3.0 %low_rank.6 = (f32[32,256]{1,0:T(8,128)S(1)}, f32[32,4096]{1,0:T(8,128)S(1)}) custom-call(bf16[64,4096]{1,0:T(8,128)(2,1)S(1)} %get-tuple-element.186.stack, bf16[256,4096]{1,0:T(8,128)(2,1)S(1)} %get-tuple-element.156.f_hi, bf16[256,4096]{1,0:T(8,128)(2,1)S(1)} %get-tuple-element.157.f_lo), custom_call_target="tpu_custom_call" | custom-call | flops 3221225472 | bytes 4194304 | tf_op jit(solution)/shard_map/low_rank/pallas_call | solution.py:353
  162.0 4.0 %step.5 = (f32[32,4096]{1,0:T(8,128)S(1)}, f32[32,4096]{1,0:T(8,128)S(1)}, bf16[64,4096]{1,0:T(8,128)(2,1)S(1)}, f32[32,128]{1,0:T(8,128)S(1)}, f32[32,256]{1,0:T(8,128)S(1)}, /*index=5*/f32[32,512]{1,0:T(8,128)S(1)}) custom-call(f32[32,2048]{1,0:T(8,128)S(1)} %constant_dynamic-update-slice_fusion.16.mine, f32[32,2048]{1,0:T(8,128)S(1)} %collective-permute-done.36.theirs, ...), custom_call_target="tpu_custom_call" | custom-call | tf_op jit(solution)/shard_map/step/pallas_call | solution.py:488
  168.5 3.0 %low_rank.7 = (f32[32,256]{1,0:T(8,128)S(1)}, f32[32,4096]{1,0:T(8,128)S(1)}) custom-call(bf16[64,4096]{1,0:T(8,128)(2,1)S(1)} %get-tuple-element.200.stack, bf16[256,4096]{1,0:T(8,128)(2,1)S(1)} %get-tuple-element.156.f_hi, bf16[256,4096]{1,0:T(8,128)(2,1)S(1)} %get-tuple-element.157.f_lo), custom_call_target="tpu_custom_call" | custom-call | flops 3221225472 | bytes 4194304 | tf_op jit(solution)/shard_map/low_rank/pallas_call | solution.py:353
  175.1 4.3 %last.1 = (bf16[64,4096]{1,0:T(8,128)(2,1)S(1)}, f32[32,128]{1,0:T(8,128)S(1)}, f32[32,256]{1,0:T(8,128)S(1)}, f32[32,128]{1,0:T(8,128)S(1)}, f32[32,128]{1,0:T(8,128)S(1)}) custom-call(f32[32,2048]{1,0:T(8,128)S(1)} %constant_dynamic-update-slice_fusion.20.mine, f32[32,2048]{1,0:T(8,128)S(1)} %collective-permute-done.40.theirs, ...), custom_call_target="tpu_custom_call" | custom-call | tf_op jit(solution)/shard_map/last/pallas_call | solution.py:488
  182.6 2.0 last_query.1
  184.6 1.6 collective-permute-done.42
  189.0 11.8 %all_to_all.11.parts = f32[16,8,128]{2,1,0:T(8,128)} all-to-all(f32[16,8,128]{2,1,0:T(8,128)} %finish.1), channel_id=1, replica_groups=mesh['dp'=16,'tensor'=8] {'dp'}, dimensions={0} | all-to-all | bytes 131072 | tf_op jit(solution)/shard_map/all_to_all | solution.py:668
  (139 shorter events, 49.3 us)
Async XLA Ops:
  6.5 96.8 %all-gather.2.cloned.1.call-start = ((), (), s32[]{:S(2)}) async-start(), calls=%async_computation.2 | async-start | bytes 8912896 | tf_op jit(solution)/shard_map/all_gather | solution.py:604
  15.6 7.2 %collective-permute-start = (f32[8,256,128]{2,1,0:T(8,128)S(1)}, f32[8,256,128]{2,1,0:T(8,128)S(1)}, u32[]{:S(2)}, u32[]{:S(2)}) collective-permute-start(f32[8,256,128]{2,1,0:T(8,128)S(1)} %project.3), channel_id=1, source_target_pairs={{0,1},{1,0},{2,3},{3,2},{4,5},{5,4},{6,7},{7,6},{8,9},{9,8},{10,11... | collective-permute-start | bytes 3145736 | tf_op jit(solution)/shard_map/ppermute | solution.py:588
  22.9 15.0 %collective-permute-start.3 = (f32[2,256,128]{2,1,0:T(8,128)S(1)}, f32[2,256,128]{2,1,0:T(8,128)S(1)}, u32[]{:S(2)}, u32[]{:S(2)}) collective-permute-start(f32[2,256,128]{2,1,0:T(8,128)S(1)} %get-tuple-element.225), channel_id=1, source_target_pairs={{0,6},{1,7},{2,0},{3,1},{4,2},{5,3},{6,4},{7,5},{8,14},{9,15},{10,... | collective-permute-start | bytes 786440 | tf_op jit(solution)/shard_map/ppermute | solution.py:611
  26.1 11.9 %collective-permute-start.2 = (f32[2,256,128]{2,1,0:T(8,128)S(1)}, f32[2,256,128]{2,1,0:T(8,128)S(1)}, u32[]{:S(2)}, u32[]{:S(2)}) collective-permute-start(f32[2,256,128]{2,1,0:T(8,128)S(1)} %get-tuple-element.226), channel_id=1, source_target_pairs={{0,4},{1,5},{2,6},{3,7},{4,0},{5,1},{6,2},{7,3},{8,12},{9,13},{10,... | collective-permute-start | bytes 786440 | tf_op jit(solution)/shard_map/ppermute | solution.py:611
  26.7 14.9 %collective-permute-start.1 = (f32[2,256,128]{2,1,0:T(8,128)S(1)}, f32[2,256,128]{2,1,0:T(8,128)S(1)}, u32[]{:S(2)}, u32[]{:S(2)}) collective-permute-start(f32[2,256,128]{2,1,0:T(8,128)S(1)} %get-tuple-element.227), channel_id=1, source_target_pairs={{0,2},{1,3},{2,4},{3,5},{4,6},{5,7},{6,0},{7,1},{8,10},{9,11},{10,... | collective-permute-start | bytes 786440 | tf_op jit(solution)/shard_map/ppermute | solution.py:611
  43.4 6.3 %collective-permute-start.6 = (f32[2,4096]{1,0:T(2,128)}, f32[2,4096]{1,0:T(2,128)S(1)}, u32[]{:S(2)}, u32[]{:S(2)}) collective-permute-start(f32[2,4096]{1,0:T(2,128)} %factor.1), channel_id=1, source_target_pairs={{0,24},{1,7},{2,26},{3,1},{4,28},{5,3},{6,30},{7,5},{8,0},{9,15},{... | collective-permute-start | bytes 98312 | tf_op jit(solution)/shard_map/ppermute | solution.py:584
  47.4 6.3 %collective-permute-start.5 = (f32[2,4096]{1,0:T(2,128)}, f32[2,4096]{1,0:T(2,128)S(1)}, u32[]{:S(2)}, u32[]{:S(2)}) collective-permute-start(f32[2,4096]{1,0:T(2,128)} %factor.1), channel_id=1, source_target_pairs={{0,16},{1,5},{2,18},{3,7},{4,20},{5,1},{6,22},{7,3},{8,24},{9,13},... | collective-permute-start | bytes 98312 | tf_op jit(solution)/shard_map/ppermute | solution.py:584
  47.4 6.4 %collective-permute-start.4 = (f32[2,4096]{1,0:T(2,128)}, f32[2,4096]{1,0:T(2,128)S(1)}, u32[]{:S(2)}, u32[]{:S(2)}) collective-permute-start(f32[2,4096]{1,0:T(2,128)} %factor.1), channel_id=1, source_target_pairs={{0,8},{1,3},{2,10},{3,5},{4,12},{5,7},{6,14},{7,1},{8,16},{9,11},{... | collective-permute-start | bytes 98312 | tf_op jit(solution)/shard_map/ppermute | solution.py:584
  54.6 18.6 %collective-permute-start.9 = (f32[8,4096]{1,0:T(8,128)S(1)}, f32[8,4096]{1,0:T(8,128)S(1)}, u32[]{:S(2)}, u32[]{:S(2)}) collective-permute-start(f32[8,4096]{1,0:T(8,128)S(1)} %pad_maximum_fusion), channel_id=1, source_target_pairs={{0,96},{1,25},{2,98},{3,27},{4,100},{5,29},{6,102},{7,31},{8,104},... | collective-permute-start | bytes 393224 | tf_op jit(solution)/shard_map/ppermute | solution.py:584
  57.4 15.8 %collective-permute-start.8 = (f32[8,4096]{1,0:T(8,128)S(1)}, f32[8,4096]{1,0:T(8,128)S(1)}, u32[]{:S(2)}, u32[]{:S(2)}) collective-permute-start(f32[8,4096]{1,0:T(8,128)S(1)} %pad_maximum_fusion), channel_id=1, source_target_pairs={{0,64},{1,17},{2,66},{3,19},{4,68},{5,21},{6,70},{7,23},{8,72},{9,... | collective-permute-start | bytes 393224 | tf_op jit(solution)/shard_map/ppermute | solution.py:584
  58.2 15.0 %collective-permute-start.7 = (f32[8,4096]{1,0:T(8,128)S(1)}, f32[8,4096]{1,0:T(8,128)S(1)}, u32[]{:S(2)}, u32[]{:S(2)}) collective-permute-start(f32[8,4096]{1,0:T(8,128)S(1)} %pad_maximum_fusion), channel_id=1, source_target_pairs={{0,32},{1,9},{2,34},{3,11},{4,36},{5,13},{6,38},{7,15},{8,40},{9,1... | collective-permute-start | bytes 393224 | tf_op jit(solution)/shard_map/ppermute | solution.py:584
  73.3 25.3 %collective-permute-start.12 = (f32[32,4096]{1,0:T(8,128)S(1)}, f32[32,4096]{1,0:T(8,128)S(1)}, u32[]{:S(2)}, u32[]{:S(2)}) collective-permute-start(f32[32,4096]{1,0:T(8,128)S(1)} %constant_dynamic-update-slice_fusion.n0), channel_id=1, source_target_pairs={{0,6},{1,97},{2,0},{3,99},{4,2},{5,101},{6,4},{7,103},{8,14},{9,10... | collective-permute-start | bytes 1572872 | tf_op jit(solution)/shard_map/ppermute | solution.py:584
  73.7 26.7 %collective-permute-start.11 = (f32[32,4096]{1,0:T(8,128)S(1)}, f32[32,4096]{1,0:T(8,128)S(1)}, u32[]{:S(2)}, u32[]{:S(2)}) collective-permute-start(f32[32,4096]{1,0:T(8,128)S(1)} %constant_dynamic-update-slice_fusion.n0), channel_id=1, source_target_pairs={{0,2},{1,33},{2,4},{3,35},{4,6},{5,37},{6,0},{7,39},{8,10},{9,41},... | collective-permute-start | bytes 1572872 | tf_op jit(solution)/shard_map/ppermute | solution.py:584
  75.4 25.3 %collective-permute-start.10 = (f32[32,4096]{1,0:T(8,128)S(1)}, f32[32,4096]{1,0:T(8,128)S(1)}, u32[]{:S(2)}, u32[]{:S(2)}) collective-permute-start(f32[32,4096]{1,0:T(8,128)S(1)} %constant_dynamic-update-slice_fusion.n0), channel_id=1, source_target_pairs={{0,4},{1,65},{2,6},{3,67},{4,0},{5,69},{6,2},{7,71},{8,12},{9,73},... | collective-permute-start | bytes 1572872 | tf_op jit(solution)/shard_map/ppermute | solution.py:584
  77.1 15.3 %collective-permute-start.16 = (f32[16,8,256]{2,1,0:T(8,128)S(1)}, f32[16,8,256]{2,1,0:T(8,128)S(1)}, u32[]{:S(2)}, u32[]{:S(2)}) collective-permute-start(f32[16,8,256]{2,1,0:T(8,128)S(1)} %maximum_select_fusion.b0), channel_id=1, source_target_pairs={{0,6},{1,7},{2,0},{3,1},{4,2},{5,3},{6,4},{7,5},{8,14},{9,15},{10,... | collective-permute-start | bytes 393224 | tf_op jit(solution)/shard_map/ppermute | solution.py:592
  79.4 13.0 %collective-permute-start.15 = (f32[16,8,256]{2,1,0:T(8,128)S(1)}, f32[16,8,256]{2,1,0:T(8,128)S(1)}, u32[]{:S(2)}, u32[]{:S(2)}) collective-permute-start(f32[16,8,256]{2,1,0:T(8,128)S(1)} %maximum_select_fusion.b0), channel_id=1, source_target_pairs={{0,4},{1,5},{2,6},{3,7},{4,0},{5,1},{6,2},{7,3},{8,12},{9,13},{10,... | collective-permute-start | bytes 393224 | tf_op jit(solution)/shard_map/ppermute | solution.py:592
  92.4 6.2 %collective-permute-start.14 = (f32[16,8,256]{2,1,0:T(8,128)S(1)}, f32[16,8,256]{2,1,0:T(8,128)S(1)}, u32[]{:S(2)}, u32[]{:S(2)}) collective-permute-start(f32[16,8,256]{2,1,0:T(8,128)S(1)} %maximum_select_fusion.b0), channel_id=1, source_target_pairs={{0,2},{1,3},{2,4},{3,5},{4,6},{5,7},{6,0},{7,1},{8,10},{9,11},{10,... | collective-permute-start | bytes 393224 | tf_op jit(solution)/shard_map/ppermute | solution.py:592
  109.7 7.5 %collective-permute-start.23 = (f32[40,512]{1,0:T(8,128)S(1)}, f32[40,512]{1,0:T(8,128)S(1)}, u32[]{:S(2)}, u32[]{:S(2)}) collective-permute-start(f32[40,512]{1,0:T(8,128)S(1)} %get-tuple-element.144), channel_id=1, source_target_pairs={{0,6},{1,7},{2,0},{3,1},{4,2},{5,3},{6,4},{7,5},{8,14},{9,15},{10,... | collective-permute-start | bytes 245768 | tf_op jit(solution)/shard_map/ppermute | solution.py:592
  110.1 7.1 %collective-permute-start.22 = (f32[40,512]{1,0:T(8,128)S(1)}, f32[40,512]{1,0:T(8,128)S(1)}, u32[]{:S(2)}, u32[]{:S(2)}) collective-permute-start(f32[40,512]{1,0:T(8,128)S(1)} %get-tuple-element.144), channel_id=1, source_target_pairs={{0,4},{1,5},{2,6},{3,7},{4,0},{5,1},{6,2},{7,3},{8,12},{9,13},{10,... | collective-permute-start | bytes 245768 | tf_op jit(solution)/shard_map/ppermute | solution.py:592
  110.6 7.0 %collective-permute-start.21 = (f32[40,512]{1,0:T(8,128)S(1)}, f32[40,512]{1,0:T(8,128)S(1)}, u32[]{:S(2)}, u32[]{:S(2)}) collective-permute-start(f32[40,512]{1,0:T(8,128)S(1)} %get-tuple-element.144), channel_id=1, source_target_pairs={{0,2},{1,3},{2,4},{3,5},{4,6},{5,7},{6,0},{7,1},{8,10},{9,11},{10,... | collective-permute-start | bytes 245768 | tf_op jit(solution)/shard_map/ppermute | solution.py:592
  123.3 8.2 %collective-permute-start.27 = (f32[32,512]{1,0:T(8,128)S(1)}, f32[32,512]{1,0:T(8,128)S(1)}, u32[]{:S(2)}, u32[]{:S(2)}) collective-permute-start(f32[32,512]{1,0:T(8,128)S(1)} %get-tuple-element.160), channel_id=1, source_target_pairs={{0,6},{1,7},{2,0},{3,1},{4,2},{5,3},{6,4},{7,5},{8,14},{9,15},{10,... | collective-permute-start | bytes 196616 | tf_op jit(solution)/shard_map/ppermute | solution.py:592
  125.7 6.2 %collective-permute-start.26 = (f32[32,512]{1,0:T(8,128)S(1)}, f32[32,512]{1,0:T(8,128)S(1)}, u32[]{:S(2)}, u32[]{:S(2)}) collective-permute-start(f32[32,512]{1,0:T(8,128)S(1)} %get-tuple-element.160), channel_id=1, source_target_pairs={{0,4},{1,5},{2,6},{3,7},{4,0},{5,1},{6,2},{7,3},{8,12},{9,13},{10,... | collective-permute-start | bytes 196616 | tf_op jit(solution)/shard_map/ppermute | solution.py:592
  127.3 5.7 %collective-permute-start.25 = (f32[32,512]{1,0:T(8,128)S(1)}, f32[32,512]{1,0:T(8,128)S(1)}, u32[]{:S(2)}, u32[]{:S(2)}) collective-permute-start(f32[32,512]{1,0:T(8,128)S(1)} %get-tuple-element.160), channel_id=1, source_target_pairs={{0,2},{1,3},{2,4},{3,5},{4,6},{5,7},{6,0},{7,1},{8,10},{9,11},{10,... | collective-permute-start | bytes 196616 | tf_op jit(solution)/shard_map/ppermute | solution.py:592
  138.6 5.7 %collective-permute-start.31 = (f32[32,512]{1,0:T(8,128)S(1)}, f32[32,512]{1,0:T(8,128)S(1)}, u32[]{:S(2)}, u32[]{:S(2)}) collective-permute-start(f32[32,512]{1,0:T(8,128)S(1)} %get-tuple-element.175), channel_id=1, source_target_pairs={{0,6},{1,7},{2,0},{3,1},{4,2},{5,3},{6,4},{7,5},{8,14},{9,15},{10,... | collective-permute-start | bytes 196616 | tf_op jit(solution)/shard_map/ppermute | solution.py:592
  139.2 5.9 %collective-permute-start.30 = (f32[32,512]{1,0:T(8,128)S(1)}, f32[32,512]{1,0:T(8,128)S(1)}, u32[]{:S(2)}, u32[]{:S(2)}) collective-permute-start(f32[32,512]{1,0:T(8,128)S(1)} %get-tuple-element.175), channel_id=1, source_target_pairs={{0,4},{1,5},{2,6},{3,7},{4,0},{5,1},{6,2},{7,3},{8,12},{9,13},{10,... | collective-permute-start | bytes 196616 | tf_op jit(solution)/shard_map/ppermute | solution.py:592
  140.6 5.5 %collective-permute-start.29 = (f32[32,512]{1,0:T(8,128)S(1)}, f32[32,512]{1,0:T(8,128)S(1)}, u32[]{:S(2)}, u32[]{:S(2)}) collective-permute-start(f32[32,512]{1,0:T(8,128)S(1)} %get-tuple-element.175), channel_id=1, source_target_pairs={{0,2},{1,3},{2,4},{3,5},{4,6},{5,7},{6,0},{7,1},{8,10},{9,11},{10,... | collective-permute-start | bytes 196616 | tf_op jit(solution)/shard_map/ppermute | solution.py:592
  152.0 6.2 %collective-permute-start.35 = (f32[32,512]{1,0:T(8,128)S(1)}, f32[32,512]{1,0:T(8,128)S(1)}, u32[]{:S(2)}, u32[]{:S(2)}) collective-permute-start(f32[32,512]{1,0:T(8,128)S(1)} %get-tuple-element.189), channel_id=1, source_target_pairs={{0,6},{1,7},{2,0},{3,1},{4,2},{5,3},{6,4},{7,5},{8,14},{9,15},{10,... | collective-permute-start | bytes 196616 | tf_op jit(solution)/shard_map/ppermute | solution.py:592
  153.5 6.2 %collective-permute-start.34 = (f32[32,512]{1,0:T(8,128)S(1)}, f32[32,512]{1,0:T(8,128)S(1)}, u32[]{:S(2)}, u32[]{:S(2)}) collective-permute-start(f32[32,512]{1,0:T(8,128)S(1)} %get-tuple-element.189), channel_id=1, source_target_pairs={{0,4},{1,5},{2,6},{3,7},{4,0},{5,1},{6,2},{7,3},{8,12},{9,13},{10,... | collective-permute-start | bytes 196616 | tf_op jit(solution)/shard_map/ppermute | solution.py:592
  154.4 5.9 %collective-permute-start.33 = (f32[32,512]{1,0:T(8,128)S(1)}, f32[32,512]{1,0:T(8,128)S(1)}, u32[]{:S(2)}, u32[]{:S(2)}) collective-permute-start(f32[32,512]{1,0:T(8,128)S(1)} %get-tuple-element.189), channel_id=1, source_target_pairs={{0,2},{1,3},{2,4},{3,5},{4,6},{5,7},{6,0},{7,1},{8,10},{9,11},{10,... | collective-permute-start | bytes 196616 | tf_op jit(solution)/shard_map/ppermute | solution.py:592
  165.9 5.5 %collective-permute-start.39 = (f32[32,512]{1,0:T(8,128)S(1)}, f32[32,512]{1,0:T(8,128)S(1)}, u32[]{:S(2)}, u32[]{:S(2)}) collective-permute-start(f32[32,512]{1,0:T(8,128)S(1)} %get-tuple-element.203), channel_id=1, source_target_pairs={{0,6},{1,7},{2,0},{3,1},{4,2},{5,3},{6,4},{7,5},{8,14},{9,15},{10,... | collective-permute-start | bytes 196616 | tf_op jit(solution)/shard_map/ppermute | solution.py:592
  166.7 6.0 %collective-permute-start.38 = (f32[32,512]{1,0:T(8,128)S(1)}, f32[32,512]{1,0:T(8,128)S(1)}, u32[]{:S(2)}, u32[]{:S(2)}) collective-permute-start(f32[32,512]{1,0:T(8,128)S(1)} %get-tuple-element.203), channel_id=1, source_target_pairs={{0,4},{1,5},{2,6},{3,7},{4,0},{5,1},{6,2},{7,3},{8,12},{9,13},{10,... | collective-permute-start | bytes 196616 | tf_op jit(solution)/shard_map/ppermute | solution.py:592
  167.8 5.7 %collective-permute-start.37 = (f32[32,512]{1,0:T(8,128)S(1)}, f32[32,512]{1,0:T(8,128)S(1)}, u32[]{:S(2)}, u32[]{:S(2)}) collective-permute-start(f32[32,512]{1,0:T(8,128)S(1)} %get-tuple-element.203), channel_id=1, source_target_pairs={{0,2},{1,3},{2,4},{3,5},{4,6},{5,7},{6,0},{7,1},{8,10},{9,11},{10,... | collective-permute-start | bytes 196616 | tf_op jit(solution)/shard_map/ppermute | solution.py:592
  (28 other events, 172.8 us)
Sparse Core Ops, SparseCore 0:
  9.5 83.3 all-gather.1

commit v2 on v1

--- a/solution.py
+++ b/solution.py
@@ -85,7 +85,7 @@
     return [(i, i ^ 1) for i in range(8)]
 
 
-ORDER = ("zxy", "yzx")
+ORDER = ("yzx", "yxz")
 
 
 def shifted(step, stage):
@@ -518,9 +518,9 @@
     side = lax.rem(core + row // 128, CORES)
     third, second, first, last = row // 32 % 4, row // 8 % 4, row // 2 % 4, row % 2
     even = 1 - side
-    dx = even * second + side * third
-    dz = even * first + side * second
-    dy = even * third + side * first
+    dx = even * third + side * second
+    dz = even * second + side * third
+    dy = first
     home = lax.rem(x + SIDE - dx, SIDE) * SIDE + lax.rem(z + SIDE - dz, SIDE)
     rank = home * 16 + side * 8 + lax.rem(y + SIDE - dy, SIDE) * 2 + last
     own[...] = exact(both, (rank == iota((rollouts, rollouts), 1)).astype(F32), NN)

time: 210 us -> 208 us (level)
    ppermute x21, waiting for transfers between devices: 27.3 us -> 23 us  [over_y(): lax.ppermute(value, 'tensor', along_y(d))]
    ppermute x9, waiting for transfers between devices: 5.09 us -> 9.31 us  [over_stage(): lax.ppermute(value, BOTH, shifted(d, stage))]
  transfers between devices with their start and end apart: 46 -> 46, of which waited for: 28 -> 28; matrix products, arithmetic and copies ran while one was open for 1% -> 1% of each run, Pallas kernels for 17% -> 18%
where the time goes in v2:
time: 208 us
  Pallas kernels  67.2 us (32%)
  waiting for transfers between devices  56.4 us (27%)
  starting transfers between devices  40.4 us (19%)
  blocking collectives  26.9 us (13%)
  between operations  13.9 us (7%)
  local copies, waits for them, and re-layouts  2.18 us (1%)
    ppermute x21, waiting for transfers between devices, over_y(): lax.ppermute(value, 'tensor', along_y(d))  23 us
    ppermute x21, starting transfers between devices, over_y(): lax.ppermute(value, 'tensor', along_y(d))  22.5 us
    pallas_call x5, Pallas kernels, cg_call(): pl.pallas_call(kernel, out_shape=outs, in_specs=[VMEM] * len(operands), o...  20.1 us
    pallas_call x2, Pallas kernels, project(): pl.pallas_call(functools.partial(project_kernel, flip=flip), out_shape=ja...  14.2 us
    all_to_all x1, blocking collectives, per_device(): start_here = lax.all_to_all(start_here, 'dp', 0, 0, tiled=True)  13.9 us
    ppermute x3, waiting for transfers between devices, per_device(): lax.ppermute(v, 'tensor', along_y(d))  13.9 us
    all_to_all x1, blocking collectives, per_device(): return place_scores(lax.all_to_all(parts, 'dp', 0, 0, tiled=True))  12.9 us
    pallas_call x4, Pallas kernels, low_rank_step(): pl.pallas_call(low_rank, out_shape=(sds((COLS, 256), F32), sds((COLS, n),...  11.9 us
  transfers between devices with their start and end apart: 46, of which 28 were waited for; matrix products, arithmetic and copies ran while one was open for 1% of the time, Pallas kernels for 18%

profile of v2, /device:TPU:0, one launch (start us, length us, event | category | flops | bytes accessed | tf_op | source)
XLA Modules:
  0.0 208.0 jit_solution(11985250609063960612)
XLA Ops:
  6.5 1.8 own_slab.1
  8.4 7.1 %project.3 = f32[8,256,128]{2,1,0:T(8,128)S(1)} custom-call(s32[14]{0:T(128)S(1)} %copy-done, s32[4]{0:T(128)S(1)} %copy-done.1, bf16[16,256,1792]{2,1,0:T(8,128)(2,1)} %act.3, bf16[16,256,512]{2,1,0:T(8,128)(2,1)} %grad.3, bf16[16,64,128]{2,1,0:T(8,128)(2,1)} %bitcast.3, bf16[16,64,128]{2,1,0:T(8,128)(2,1)} %bitcast.5), custom_call_target="tpu_custom_call" | custom-call | flops 2415919104 | bytes 9437184 | tf_op jit(solution)/shard_map/project/pallas_call | solution.py:133
  15.7 7.1 %project.2 = f32[8,256,128]{2,1,0:T(8,128)S(1)} custom-call(s32[14]{0:T(128)S(1)} %copy-done, s32[4]{0:T(128)S(1)} %copy-done.1, bf16[16,256,1792]{2,1,0:T(8,128)(2,1)} %act.3, bf16[16,256,512]{2,1,0:T(8,128)(2,1)} %grad.3, bf16[16,64,128]{2,1,0:T(8,128)(2,1)} %bitcast.4, bf16[16,64,128]{2,1,0:T(8,128)(2,1)} %bitcast.6), custom_call_target="tpu_custom_call" | custom-call | flops 2415919104 | bytes 9437184 | tf_op jit(solution)/shard_map/project/pallas_call | solution.py:133
  22.9 3.2 %collective-permute-start.3 = (f32[2,256,128]{2,1,0:T(8,128)S(1)}, f32[2,256,128]{2,1,0:T(8,128)S(1)}, u32[]{:S(2)}, u32[]{:S(2)}) collective-permute-start(f32[2,256,128]{2,1,0:T(8,128)S(1)} %get-tuple-element.225), channel_id=1, source_target_pairs={{0,6},{1,7},{2,0},{3,1},{4,2},{5,3},{6,4},{7,5},{8,14},{9,15},{10,... | collective-permute-start | bytes 786440 | tf_op jit(solution)/shard_map/ppermute | solution.py:611
  27.7 10.2 %collective-permute-done.3.w3 = f32[2,256,128]{2,1,0:T(8,128)S(1)} collective-permute-done((f32[2,256,128]{2,1,0:T(8,128)S(1)}, f32[2,256,128]{2,1,0:T(8,128)S(1)}, u32[]{:S(2)}, u32[]{:S(2)}) %collective-permute-start.3) | collective-permute-done | bytes 262176 | tf_op jit(solution)/shard_map/ppermute | solution.py:611
  37.9 3.7 %collective-permute-done.1.w1 = f32[2,256,128]{2,1,0:T(8,128)S(1)} collective-permute-done((f32[2,256,128]{2,1,0:T(8,128)S(1)}, f32[2,256,128]{2,1,0:T(8,128)S(1)}, u32[]{:S(2)}, u32[]{:S(2)}) %collective-permute-start.1) | collective-permute-done | bytes 262176 | tf_op jit(solution)/shard_map/ppermute | solution.py:611
  41.6 1.7 factor.1
  45.4 2.0 collective-permute-done.6
  47.5 2.1 %collective-permute-done.5 = f32[2,4096]{1,0:T(2,128)S(1)} collective-permute-done((f32[2,4096]{1,0:T(2,128)}, f32[2,4096]{1,0:T(2,128)S(1)}, u32[]{:S(2)}, u32[]{:S(2)}) %collective-permute-start.5) | collective-permute-done | bytes 32800 | tf_op jit(solution)/shard_map/ppermute | solution.py:584
  51.0 4.1 %collective-permute-start.9 = (f32[8,4096]{1,0:T(8,128)S(1)}, f32[8,4096]{1,0:T(8,128)S(1)}, u32[]{:S(2)}, u32[]{:S(2)}) collective-permute-start(f32[8,4096]{1,0:T(8,128)S(1)} %pad_maximum_fusion), channel_id=1, source_target_pairs={{0,24},{1,97},{2,26},{3,99},{4,28},{5,101},{6,30},{7,103},{8,0},{9... | collective-permute-start | bytes 393224 | tf_op jit(solution)/shard_map/ppermute | solution.py:584
  56.4 13.9 %all_to_all.10 = f32[16,4,256]{2,1,0:T(4,128)S(1)} all-to-all(f32[16,4,256]{2,1,0:T(4,128)S(1)} %reshape.3), channel_id=1, replica_groups=mesh['dp'=16,'tensor'=8] {'dp'}, dimensions={0} | all-to-all | bytes 131072 | tf_op jit(solution)/shard_map/all_to_all | solution.py:616
  70.4 1.8 collective-permute-start.12
  72.5 2.0 collective-permute-start.10
  75.9 2.1 collective-permute-start.16
  78.9 5.0 %collective-permute-done.16.b3 = f32[16,8,256]{2,1,0:T(8,128)S(1)} collective-permute-done((f32[16,8,256]{2,1,0:T(8,128)S(1)}, f32[16,8,256]{2,1,0:T(8,128)S(1)}, u32[]{:S(2)}, u32[]{:S(2)}) %collective-permute-start.16) | collective-permute-done | bytes 131104 | tf_op jit(solution)/shard_map/ppermute | solution.py:592
  84.7 5.7 %collective-permute-done.14.b1 = f32[16,8,256]{2,1,0:T(8,128)S(1)} collective-permute-done((f32[16,8,256]{2,1,0:T(8,128)S(1)}, f32[16,8,256]{2,1,0:T(8,128)S(1)}, u32[]{:S(2)}, u32[]{:S(2)}) %collective-permute-start.14) | collective-permute-done | bytes 131104 | tf_op jit(solution)/shard_map/ppermute | solution.py:592
  92.6 4.5 %collective-permute-done.10.n2 = f32[32,4096]{1,0:T(8,128)S(1)} collective-permute-done((f32[32,4096]{1,0:T(8,128)S(1)}, f32[32,4096]{1,0:T(8,128)S(1)}, u32[]{:S(2)}, u32[]{:S(2)}) %collective-permute-start.10) | collective-permute-done | bytes 524320 | tf_op jit(solution)/shard_map/ppermute | solution.py:584
  99.2 6.3 %prior_image.1 = (bf16[512,4096]{1,0:T(8,128)(2,1)S(1)}, bf16[512,4096]{1,0:T(8,128)(2,1)S(1)}, f32[40,512]{1,0:T(8,128)S(1)}) custom-call(bf16[64,4096]{1,0:T(8,128)(2,1)S(1)} %get-tuple-element.132.stack, f32[512,4096]{1,0:T(8,128)} %all-gather.2.cloned.1.call-done.prior_hbm), custom_call_target="tpu_custom_call" | custom-call | flops 3221225472 | bytes 16777216 | tf_op jit(solution)/shard_map/prior_image/pallas_call | solution.py:290
  105.5 2.8 %collective-permute-start.23 = (f32[40,512]{1,0:T(8,128)S(1)}, f32[40,512]{1,0:T(8,128)S(1)}, u32[]{:S(2)}, u32[]{:S(2)}) collective-permute-start(f32[40,512]{1,0:T(8,128)S(1)} %get-tuple-element.144), channel_id=1, source_target_pairs={{0,6},{1,7},{2,0},{3,1},{4,2},{5,3},{6,4},{7,5},{8,14},{9,15},{10,... | collective-permute-start | bytes 245768 | tf_op jit(solution)/shard_map/ppermute | solution.py:592
  110.0 5.4 %take_factors.1 = (bf16[256,4096]{1,0:T(8,128)(2,1)S(1)}, bf16[256,4096]{1,0:T(8,128)(2,1)S(1)}, f32[32,256]{1,0:T(8,128)S(1)}, f32[32,4096]{1,0:T(8,128)S(1)}, f32[8,128]{1,0:T(8,128)S(1)}) custom-call(f32[32,4096]{1,0:T(8,128)} %copy-done.7, f32[32,4096]{1,0:T(8,128)} %copy-done.9, f32[32,4096]{1,0:T(8,128)} %copy-done.10, f32[32,4096]{1,0:T(8,128)} %copy-done.8, ...), custom_call_target="tpu_custom_call" | custom-call | flops 3221225472 | bytes 8388608 | tf_op jit(solution)/shard_map/take_factors/pallas_call | solution.py:335
  117.7 4.0 %first.1 = (f32[32,4096]{1,0:T(8,128)S(1)}, f32[32,4096]{1,0:T(8,128)S(1)}, bf16[64,4096]{1,0:T(8,128)(2,1)S(1)}, f32[32,128]{1,0:T(8,128)S(1)}, f32[32,256]{1,0...) custom-call(f32[40,2048]{1,0:T(8,128)S(1)} %constant_dynamic-update-slice_fusion.4.mine, ...), custom_call_target="tpu_custom_call" | custom-call | tf_op jit(solution)/shard_map/first/pallas_call | solution.py:488
  121.7 2.0 collective-permute-start.27
  125.1 3.0 %low_rank.4 = (f32[32,256]{1,0:T(8,128)S(1)}, f32[32,4096]{1,0:T(8,128)S(1)}) custom-call(bf16[64,4096]{1,0:T(8,128)(2,1)S(1)} %get-tuple-element.155.stack, bf16[256,4096]{1,0:T(8,128)(2,1)S(1)} %get-tuple-element.156.f_hi, bf16[256,4096]{1,0:T(8,128)(2,1)S(1)} %get-tuple-element.157.f_lo), custom_call_target="tpu_custom_call" | custom-call | flops 3221225472 | bytes 4194304 | tf_op jit(solution)/shard_map/low_rank/pallas_call | solution.py:353
  132.3 4.0 %step.3 = (f32[32,4096]{1,0:T(8,128)S(1)}, f32[32,4096]{1,0:T(8,128)S(1)}, bf16[64,4096]{1,0:T(8,128)(2,1)S(1)}, f32[32,128]{1,0:T(8,128)S(1)}, f32[32,256]{1,0:T(8,128)S(1)}, /*index=5*/f32[32,512]{1,0:T(8,128)S(1)}) custom-call(f32[32,2048]{1,0:T(8,128)S(1)} %constant_dynamic-update-slice_fusion.8.mine, f32[32,2048]{1,0:T(8,128)S(1)} %collective-permute-done.28.theirs, ...), custom_call_target="tpu_custom_call" | custom-call | tf_op jit(solution)/shard_map/step/pallas_call | solution.py:488
  139.0 3.0 %low_rank.5 = (f32[32,256]{1,0:T(8,128)S(1)}, f32[32,4096]{1,0:T(8,128)S(1)}) custom-call(bf16[64,4096]{1,0:T(8,128)(2,1)S(1)} %get-tuple-element.172.stack, bf16[256,4096]{1,0:T(8,128)(2,1)S(1)} %get-tuple-element.156.f_hi, bf16[256,4096]{1,0:T(8,128)(2,1)S(1)} %get-tuple-element.157.f_lo), custom_call_target="tpu_custom_call" | custom-call | flops 3221225472 | bytes 4194304 | tf_op jit(solution)/shard_map/low_rank/pallas_call | solution.py:353
  145.7 4.0 %step.4 = (f32[32,4096]{1,0:T(8,128)S(1)}, f32[32,4096]{1,0:T(8,128)S(1)}, bf16[64,4096]{1,0:T(8,128)(2,1)S(1)}, f32[32,128]{1,0:T(8,128)S(1)}, f32[32,256]{1,0:T(8,128)S(1)}, /*index=5*/f32[32,512]{1,0:T(8,128)S(1)}) custom-call(f32[32,2048]{1,0:T(8,128)S(1)} %constant_dynamic-update-slice_fusion.12.mine, f32[32,2048]{1,0:T(8,128)S(1)} %collective-permute-done.32.theirs, ...), custom_call_target="tpu_custom_call" | custom-call | tf_op jit(solution)/shard_map/step/pallas_call | solution.py:488
  152.8 3.0 %low_rank.6 = (f32[32,256]{1,0:T(8,128)S(1)}, f32[32,4096]{1,0:T(8,128)S(1)}) custom-call(bf16[64,4096]{1,0:T(8,128)(2,1)S(1)} %get-tuple-element.186.stack, bf16[256,4096]{1,0:T(8,128)(2,1)S(1)} %get-tuple-element.156.f_hi, bf16[256,4096]{1,0:T(8,128)(2,1)S(1)} %get-tuple-element.157.f_lo), custom_call_target="tpu_custom_call" | custom-call | flops 3221225472 | bytes 4194304 | tf_op jit(solution)/shard_map/low_rank/pallas_call | solution.py:353
  159.6 4.0 %step.5 = (f32[32,4096]{1,0:T(8,128)S(1)}, f32[32,4096]{1,0:T(8,128)S(1)}, bf16[64,4096]{1,0:T(8,128)(2,1)S(1)}, f32[32,128]{1,0:T(8,128)S(1)}, f32[32,256]{1,0:T(8,128)S(1)}, /*index=5*/f32[32,512]{1,0:T(8,128)S(1)}) custom-call(f32[32,2048]{1,0:T(8,128)S(1)} %constant_dynamic-update-slice_fusion.16.mine, f32[32,2048]{1,0:T(8,128)S(1)} %collective-permute-done.36.theirs, ...), custom_call_target="tpu_custom_call" | custom-call | tf_op jit(solution)/shard_map/step/pallas_call | solution.py:488
  166.1 3.0 %low_rank.7 = (f32[32,256]{1,0:T(8,128)S(1)}, f32[32,4096]{1,0:T(8,128)S(1)}) custom-call(bf16[64,4096]{1,0:T(8,128)(2,1)S(1)} %get-tuple-element.200.stack, bf16[256,4096]{1,0:T(8,128)(2,1)S(1)} %get-tuple-element.156.f_hi, bf16[256,4096]{1,0:T(8,128)(2,1)S(1)} %get-tuple-element.157.f_lo), custom_call_target="tpu_custom_call" | custom-call | flops 3221225472 | bytes 4194304 | tf_op jit(solution)/shard_map/low_rank/pallas_call | solution.py:353
  172.9 4.3 %last.1 = (bf16[64,4096]{1,0:T(8,128)(2,1)S(1)}, f32[32,128]{1,0:T(8,128)S(1)}, f32[32,256]{1,0:T(8,128)S(1)}, f32[32,128]{1,0:T(8,128)S(1)}, f32[32,128]{1,0:T(8,128)S(1)}) custom-call(f32[32,2048]{1,0:T(8,128)S(1)} %constant_dynamic-update-slice_fusion.20.mine, f32[32,2048]{1,0:T(8,128)S(1)} %collective-permute-done.40.theirs, ...), custom_call_target="tpu_custom_call" | custom-call | tf_op jit(solution)/shard_map/last/pallas_call | solution.py:488
  180.3 2.0 last_query.1
  186.7 12.9 %all_to_all.11.parts = f32[16,8,128]{2,1,0:T(8,128)} all-to-all(f32[16,8,128]{2,1,0:T(8,128)} %finish.1), channel_id=1, replica_groups=mesh['dp'=16,'tensor'=8] {'dp'}, dimensions={0} | all-to-all | bytes 131072 | tf_op jit(solution)/shard_map/all_to_all | solution.py:668
  (139 shorter events, 52.4 us)
Async XLA Ops:
  6.5 92.6 %all-gather.2.cloned.1.call-start = ((), (), s32[]{:S(2)}) async-start(), calls=%async_computation.2 | async-start | bytes 8912896 | tf_op jit(solution)/shard_map/all_gather | solution.py:604
  15.6 7.2 %collective-permute-start = (f32[8,256,128]{2,1,0:T(8,128)S(1)}, f32[8,256,128]{2,1,0:T(8,128)S(1)}, u32[]{:S(2)}, u32[]{:S(2)}) collective-permute-start(f32[8,256,128]{2,1,0:T(8,128)S(1)} %project.3), channel_id=1, source_target_pairs={{0,1},{1,0},{2,3},{3,2},{4,5},{5,4},{6,7},{7,6},{8,9},{9,8},{10,11... | collective-permute-start | bytes 3145736 | tf_op jit(solution)/shard_map/ppermute | solution.py:588
  22.9 15.0 %collective-permute-start.3 = (f32[2,256,128]{2,1,0:T(8,128)S(1)}, f32[2,256,128]{2,1,0:T(8,128)S(1)}, u32[]{:S(2)}, u32[]{:S(2)}) collective-permute-start(f32[2,256,128]{2,1,0:T(8,128)S(1)} %get-tuple-element.225), channel_id=1, source_target_pairs={{0,6},{1,7},{2,0},{3,1},{4,2},{5,3},{6,4},{7,5},{8,14},{9,15},{10,... | collective-permute-start | bytes 786440 | tf_op jit(solution)/shard_map/ppermute | solution.py:611
  26.1 11.8 %collective-permute-start.2 = (f32[2,256,128]{2,1,0:T(8,128)S(1)}, f32[2,256,128]{2,1,0:T(8,128)S(1)}, u32[]{:S(2)}, u32[]{:S(2)}) collective-permute-start(f32[2,256,128]{2,1,0:T(8,128)S(1)} %get-tuple-element.226), channel_id=1, source_target_pairs={{0,4},{1,5},{2,6},{3,7},{4,0},{5,1},{6,2},{7,3},{8,12},{9,13},{10,... | collective-permute-start | bytes 786440 | tf_op jit(solution)/shard_map/ppermute | solution.py:611
  26.7 14.9 %collective-permute-start.1 = (f32[2,256,128]{2,1,0:T(8,128)S(1)}, f32[2,256,128]{2,1,0:T(8,128)S(1)}, u32[]{:S(2)}, u32[]{:S(2)}) collective-permute-start(f32[2,256,128]{2,1,0:T(8,128)S(1)} %get-tuple-element.227), channel_id=1, source_target_pairs={{0,2},{1,3},{2,4},{3,5},{4,6},{5,7},{6,0},{7,1},{8,10},{9,11},{10,... | collective-permute-start | bytes 786440 | tf_op jit(solution)/shard_map/ppermute | solution.py:611
  44.0 5.6 %collective-permute-start.5 = (f32[2,4096]{1,0:T(2,128)}, f32[2,4096]{1,0:T(2,128)S(1)}, u32[]{:S(2)}, u32[]{:S(2)}) collective-permute-start(f32[2,4096]{1,0:T(2,128)} %factor.1), channel_id=1, source_target_pairs={{0,4},{1,5},{2,6},{3,7},{4,0},{5,1},{6,2},{7,3},{8,12},{9,13},{10,... | collective-permute-start | bytes 98312 | tf_op jit(solution)/shard_map/ppermute | solution.py:584
  44.6 5.6 %collective-permute-start.4 = (f32[2,4096]{1,0:T(2,128)}, f32[2,4096]{1,0:T(2,128)S(1)}, u32[]{:S(2)}, u32[]{:S(2)}) collective-permute-start(f32[2,4096]{1,0:T(2,128)} %factor.1), channel_id=1, source_target_pairs={{0,2},{1,3},{2,4},{3,5},{4,6},{5,7},{6,0},{7,1},{8,10},{9,11},{10,... | collective-permute-start | bytes 98312 | tf_op jit(solution)/shard_map/ppermute | solution.py:584
  51.0 19.3 %collective-permute-start.9 = (f32[8,4096]{1,0:T(8,128)S(1)}, f32[8,4096]{1,0:T(8,128)S(1)}, u32[]{:S(2)}, u32[]{:S(2)}) collective-permute-start(f32[8,4096]{1,0:T(8,128)S(1)} %pad_maximum_fusion), channel_id=1, source_target_pairs={{0,24},{1,97},{2,26},{3,99},{4,28},{5,101},{6,30},{7,103},{8,0},{9... | collective-permute-start | bytes 393224 | tf_op jit(solution)/shard_map/ppermute | solution.py:584
  55.1 15.2 %collective-permute-start.8 = (f32[8,4096]{1,0:T(8,128)S(1)}, f32[8,4096]{1,0:T(8,128)S(1)}, u32[]{:S(2)}, u32[]{:S(2)}) collective-permute-start(f32[8,4096]{1,0:T(8,128)S(1)} %pad_maximum_fusion), channel_id=1, source_target_pairs={{0,16},{1,65},{2,18},{3,67},{4,20},{5,69},{6,22},{7,71},{8,24},{9,... | collective-permute-start | bytes 393224 | tf_op jit(solution)/shard_map/ppermute | solution.py:584
  55.1 15.2 %collective-permute-start.7 = (f32[8,4096]{1,0:T(8,128)S(1)}, f32[8,4096]{1,0:T(8,128)S(1)}, u32[]{:S(2)}, u32[]{:S(2)}) collective-permute-start(f32[8,4096]{1,0:T(8,128)S(1)} %pad_maximum_fusion), channel_id=1, source_target_pairs={{0,8},{1,33},{2,10},{3,35},{4,12},{5,37},{6,14},{7,39},{8,16},{9,4... | collective-permute-start | bytes 393224 | tf_op jit(solution)/shard_map/ppermute | solution.py:584
  70.4 20.0 %collective-permute-start.12 = (f32[32,4096]{1,0:T(8,128)S(1)}, f32[32,4096]{1,0:T(8,128)S(1)}, u32[]{:S(2)}, u32[]{:S(2)}) collective-permute-start(f32[32,4096]{1,0:T(8,128)S(1)} %constant_dynamic-update-slice_fusion.n0), channel_id=1, source_target_pairs={{0,96},{1,25},{2,98},{3,27},{4,100},{5,29},{6,102},{7,31},{8,104},... | collective-permute-start | bytes 1572872 | tf_op jit(solution)/shard_map/ppermute | solution.py:584
  72.3 20.1 %collective-permute-start.11 = (f32[32,4096]{1,0:T(8,128)S(1)}, f32[32,4096]{1,0:T(8,128)S(1)}, u32[]{:S(2)}, u32[]{:S(2)}) collective-permute-start(f32[32,4096]{1,0:T(8,128)S(1)} %constant_dynamic-update-slice_fusion.n0), channel_id=1, source_target_pairs={{0,32},{1,9},{2,34},{3,11},{4,36},{5,13},{6,38},{7,15},{8,40},{9,1... | collective-permute-start | bytes 1572872 | tf_op jit(solution)/shard_map/ppermute | solution.py:584
  72.5 24.6 %collective-permute-start.10 = (f32[32,4096]{1,0:T(8,128)S(1)}, f32[32,4096]{1,0:T(8,128)S(1)}, u32[]{:S(2)}, u32[]{:S(2)}) collective-permute-start(f32[32,4096]{1,0:T(8,128)S(1)} %constant_dynamic-update-slice_fusion.n0), channel_id=1, source_target_pairs={{0,64},{1,17},{2,66},{3,19},{4,68},{5,21},{6,70},{7,23},{8,72},{9,... | collective-permute-start | bytes 1572872 | tf_op jit(solution)/shard_map/ppermute | solution.py:584
  75.9 8.0 %collective-permute-start.16 = (f32[16,8,256]{2,1,0:T(8,128)S(1)}, f32[16,8,256]{2,1,0:T(8,128)S(1)}, u32[]{:S(2)}, u32[]{:S(2)}) collective-permute-start(f32[16,8,256]{2,1,0:T(8,128)S(1)} %maximum_select_fusion.b0), channel_id=1, source_target_pairs={{0,6},{1,7},{2,0},{3,1},{4,2},{5,3},{6,4},{7,5},{8,14},{9,15},{10,... | collective-permute-start | bytes 393224 | tf_op jit(solution)/shard_map/ppermute | solution.py:592
  77.9 6.8 %collective-permute-start.15 = (f32[16,8,256]{2,1,0:T(8,128)S(1)}, f32[16,8,256]{2,1,0:T(8,128)S(1)}, u32[]{:S(2)}, u32[]{:S(2)}) collective-permute-start(f32[16,8,256]{2,1,0:T(8,128)S(1)} %maximum_select_fusion.b0), channel_id=1, source_target_pairs={{0,4},{1,5},{2,6},{3,7},{4,0},{5,1},{6,2},{7,3},{8,12},{9,13},{10,... | collective-permute-start | bytes 393224 | tf_op jit(solution)/shard_map/ppermute | solution.py:592
  83.9 6.6 %collective-permute-start.14 = (f32[16,8,256]{2,1,0:T(8,128)S(1)}, f32[16,8,256]{2,1,0:T(8,128)S(1)}, u32[]{:S(2)}, u32[]{:S(2)}) collective-permute-start(f32[16,8,256]{2,1,0:T(8,128)S(1)} %maximum_select_fusion.b0), channel_id=1, source_target_pairs={{0,2},{1,3},{2,4},{3,5},{4,6},{5,7},{6,0},{7,1},{8,10},{9,11},{10,... | collective-permute-start | bytes 393224 | tf_op jit(solution)/shard_map/ppermute | solution.py:592
  90.5 6.8 %collective-permute-start.17 = (f32[32,4096]{1,0:T(8,128)S(1)}, f32[32,4096]{1,0:T(8,128)S(1)}, u32[]{:S(2)}, u32[]{:S(2)}) collective-permute-start(f32[32,4096]{1,0:T(8,128)S(1)} %constant_dynamic-update-slice_fusion.n0), channel_id=1, source_target_pairs={{0,1},{1,0},{2,3},{3,2},{4,5},{5,4},{6,7},{7,6},{8,9},{9,8},{10,11... | collective-permute-start | bytes 1572872 | tf_op jit(solution)/shard_map/ppermute | solution.py:588
  90.5 6.8 %collective-permute-start.20 = (f32[32,4096]{1,0:T(8,128)S(1)}, f32[32,4096]{1,0:T(8,128)S(1)}, u32[]{:S(2)}, u32[]{:S(2)}) collective-permute-start(f32[32,4096]{1,0:T(8,128)S(1)} %collective-permute-done.12.n3), channel_id=1, source_target_pairs={{0,1},{1,0},{2,3},{3,2},{4,5},{5,4},{6,7},{7,6},{8,9},{9,8},{10,11... | collective-permute-start | bytes 1572872 | tf_op jit(solution)/shard_map/ppermute | solution.py:588
  105.5 9.9 %collective-permute-start.23 = (f32[40,512]{1,0:T(8,128)S(1)}, f32[40,512]{1,0:T(8,128)S(1)}, u32[]{:S(2)}, u32[]{:S(2)}) collective-permute-start(f32[40,512]{1,0:T(8,128)S(1)} %get-tuple-element.144), channel_id=1, source_target_pairs={{0,6},{1,7},{2,0},{3,1},{4,2},{5,3},{6,4},{7,5},{8,14},{9,15},{10,... | collective-permute-start | bytes 245768 | tf_op jit(solution)/shard_map/ppermute | solution.py:592
  108.3 7.1 %collective-permute-start.22 = (f32[40,512]{1,0:T(8,128)S(1)}, f32[40,512]{1,0:T(8,128)S(1)}, u32[]{:S(2)}, u32[]{:S(2)}) collective-permute-start(f32[40,512]{1,0:T(8,128)S(1)} %get-tuple-element.144), channel_id=1, source_target_pairs={{0,4},{1,5},{2,6},{3,7},{4,0},{5,1},{6,2},{7,3},{8,12},{9,13},{10,... | collective-permute-start | bytes 245768 | tf_op jit(solution)/shard_map/ppermute | solution.py:592
  109.1 6.8 %collective-permute-start.21 = (f32[40,512]{1,0:T(8,128)S(1)}, f32[40,512]{1,0:T(8,128)S(1)}, u32[]{:S(2)}, u32[]{:S(2)}) collective-permute-start(f32[40,512]{1,0:T(8,128)S(1)} %get-tuple-element.144), channel_id=1, source_target_pairs={{0,2},{1,3},{2,4},{3,5},{4,6},{5,7},{6,0},{7,1},{8,10},{9,11},{10,... | collective-permute-start | bytes 245768 | tf_op jit(solution)/shard_map/ppermute | solution.py:592
  121.7 6.5 %collective-permute-start.27 = (f32[32,512]{1,0:T(8,128)S(1)}, f32[32,512]{1,0:T(8,128)S(1)}, u32[]{:S(2)}, u32[]{:S(2)}) collective-permute-start(f32[32,512]{1,0:T(8,128)S(1)} %get-tuple-element.160), channel_id=1, source_target_pairs={{0,6},{1,7},{2,0},{3,1},{4,2},{5,3},{6,4},{7,5},{8,14},{9,15},{10,... | collective-permute-start | bytes 196616 | tf_op jit(solution)/shard_map/ppermute | solution.py:592
  123.6 6.2 %collective-permute-start.26 = (f32[32,512]{1,0:T(8,128)S(1)}, f32[32,512]{1,0:T(8,128)S(1)}, u32[]{:S(2)}, u32[]{:S(2)}) collective-permute-start(f32[32,512]{1,0:T(8,128)S(1)} %get-tuple-element.160), channel_id=1, source_target_pairs={{0,4},{1,5},{2,6},{3,7},{4,0},{5,1},{6,2},{7,3},{8,12},{9,13},{10,... | collective-permute-start | bytes 196616 | tf_op jit(solution)/shard_map/ppermute | solution.py:592
  136.3 5.7 %collective-permute-start.31 = (f32[32,512]{1,0:T(8,128)S(1)}, f32[32,512]{1,0:T(8,128)S(1)}, u32[]{:S(2)}, u32[]{:S(2)}) collective-permute-start(f32[32,512]{1,0:T(8,128)S(1)} %get-tuple-element.175), channel_id=1, source_target_pairs={{0,6},{1,7},{2,0},{3,1},{4,2},{5,3},{6,4},{7,5},{8,14},{9,15},{10,... | collective-permute-start | bytes 196616 | tf_op jit(solution)/shard_map/ppermute | solution.py:592
  137.1 6.1 %collective-permute-start.30 = (f32[32,512]{1,0:T(8,128)S(1)}, f32[32,512]{1,0:T(8,128)S(1)}, u32[]{:S(2)}, u32[]{:S(2)}) collective-permute-start(f32[32,512]{1,0:T(8,128)S(1)} %get-tuple-element.175), channel_id=1, source_target_pairs={{0,4},{1,5},{2,6},{3,7},{4,0},{5,1},{6,2},{7,3},{8,12},{9,13},{10,... | collective-permute-start | bytes 196616 | tf_op jit(solution)/shard_map/ppermute | solution.py:592
  138.2 5.7 %collective-permute-start.29 = (f32[32,512]{1,0:T(8,128)S(1)}, f32[32,512]{1,0:T(8,128)S(1)}, u32[]{:S(2)}, u32[]{:S(2)}) collective-permute-start(f32[32,512]{1,0:T(8,128)S(1)} %get-tuple-element.175), channel_id=1, source_target_pairs={{0,2},{1,3},{2,4},{3,5},{4,6},{5,7},{6,0},{7,1},{8,10},{9,11},{10,... | collective-permute-start | bytes 196616 | tf_op jit(solution)/shard_map/ppermute | solution.py:592
  149.7 6.1 %collective-permute-start.35 = (f32[32,512]{1,0:T(8,128)S(1)}, f32[32,512]{1,0:T(8,128)S(1)}, u32[]{:S(2)}, u32[]{:S(2)}) collective-permute-start(f32[32,512]{1,0:T(8,128)S(1)} %get-tuple-element.189), channel_id=1, source_target_pairs={{0,6},{1,7},{2,0},{3,1},{4,2},{5,3},{6,4},{7,5},{8,14},{9,15},{10,... | collective-permute-start | bytes 196616 | tf_op jit(solution)/shard_map/ppermute | solution.py:592
  151.2 6.3 %collective-permute-start.34 = (f32[32,512]{1,0:T(8,128)S(1)}, f32[32,512]{1,0:T(8,128)S(1)}, u32[]{:S(2)}, u32[]{:S(2)}) collective-permute-start(f32[32,512]{1,0:T(8,128)S(1)} %get-tuple-element.189), channel_id=1, source_target_pairs={{0,4},{1,5},{2,6},{3,7},{4,0},{5,1},{6,2},{7,3},{8,12},{9,13},{10,... | collective-permute-start | bytes 196616 | tf_op jit(solution)/shard_map/ppermute | solution.py:592
  152.1 5.9 %collective-permute-start.33 = (f32[32,512]{1,0:T(8,128)S(1)}, f32[32,512]{1,0:T(8,128)S(1)}, u32[]{:S(2)}, u32[]{:S(2)}) collective-permute-start(f32[32,512]{1,0:T(8,128)S(1)} %get-tuple-element.189), channel_id=1, source_target_pairs={{0,2},{1,3},{2,4},{3,5},{4,6},{5,7},{6,0},{7,1},{8,10},{9,11},{10,... | collective-permute-start | bytes 196616 | tf_op jit(solution)/shard_map/ppermute | solution.py:592
  163.6 5.5 %collective-permute-start.39 = (f32[32,512]{1,0:T(8,128)S(1)}, f32[32,512]{1,0:T(8,128)S(1)}, u32[]{:S(2)}, u32[]{:S(2)}) collective-permute-start(f32[32,512]{1,0:T(8,128)S(1)} %get-tuple-element.203), channel_id=1, source_target_pairs={{0,6},{1,7},{2,0},{3,1},{4,2},{5,3},{6,4},{7,5},{8,14},{9,15},{10,... | collective-permute-start | bytes 196616 | tf_op jit(solution)/shard_map/ppermute | solution.py:592
  164.4 6.1 %collective-permute-start.38 = (f32[32,512]{1,0:T(8,128)S(1)}, f32[32,512]{1,0:T(8,128)S(1)}, u32[]{:S(2)}, u32[]{:S(2)}) collective-permute-start(f32[32,512]{1,0:T(8,128)S(1)} %get-tuple-element.203), channel_id=1, source_target_pairs={{0,4},{1,5},{2,6},{3,7},{4,0},{5,1},{6,2},{7,3},{8,12},{9,13},{10,... | collective-permute-start | bytes 196616 | tf_op jit(solution)/shard_map/ppermute | solution.py:592
  165.5 5.7 %collective-permute-start.37 = (f32[32,512]{1,0:T(8,128)S(1)}, f32[32,512]{1,0:T(8,128)S(1)}, u32[]{:S(2)}, u32[]{:S(2)}) collective-permute-start(f32[32,512]{1,0:T(8,128)S(1)} %get-tuple-element.203), channel_id=1, source_target_pairs={{0,2},{1,3},{2,4},{3,5},{4,6},{5,7},{6,0},{7,1},{8,10},{9,11},{10,... | collective-permute-start | bytes 196616 | tf_op jit(solution)/shard_map/ppermute | solution.py:592
  (28 other events, 177.1 us)
Sparse Core Ops, SparseCore 0:
  9.5 83.0 all-gather.1

commit v3 on v2

--- a/solution.py
+++ b/solution.py
@@ -316,13 +316,17 @@
 
 
 def factors_kernel(n0, n1, n2, n3, m0, m1, m2, m3, stack, f_hi, f_lo, query, low, square_out, pieces, sems):
-    copies = fetch((n0, n1, n2, n3, m0, m1, m2, m3), [pieces.at[i] for i in range(8)], sems)
+    late = (n1, n2, n3, m2,)
+    copies = fetch(late, [pieces.at[i] for i in range(len(late))], sems)
+    sources = [n0, m0, m1, m3] + [pieces.at[i] for i in range(len(late))]
+    order = (0, 4, 5, 7, 1, 2, 3, 6)
     square = jnp.zeros((32, BLK), F32)
-    for i in range(8):
-        copies[i].wait()
+    for position, (i, source) in enumerate(zip(order, sources)):
+        if position >= 4:
+            copies[position - 4].wait()
         rows = slice(i * 32, (i + 1) * 32)
         for cols in BLOCKS:
-            value = pieces[i, :, cols]
+            value = source[:, cols]
             square = square + value * value
             f_hi[rows, cols], f_lo[rows, cols] = split(value)
     square_out[...] = jnp.full(square_out.shape, jnp.sum(square), F32)
@@ -338,13 +342,13 @@
             pltpu.VMEM((256, n), BF16), pltpu.VMEM((256, n), BF16),
             sds((COLS, 256), F32), sds((COLS, n), F32), sds((8, 128), F32),
         ),
-        in_specs=[HBM] * 8 + [VMEM],
+        in_specs=[VMEM, HBM, HBM, HBM, VMEM, VMEM, HBM, VMEM, VMEM],
         out_specs=(VMEM,) * 5,
-        scratch_shapes=[pltpu.VMEM((8, 32, n), F32), pltpu.SemaphoreType.DMA((8,))],
+        scratch_shapes=[pltpu.VMEM((4, 32, n), F32), pltpu.SemaphoreType.DMA((4,))],
         compiler_params=params(20),
         cost_estimate=cost(12 * 256 * 256 * n, 8 * 256 * n),
         name="take_factors",
-    )(*in_hbm(pieces), stack)
+    )(*[(in_vmem if i in (0, 4, 5, 7,) else in_hbm)([v])[0] for i, v in enumerate(pieces)], stack)
 
 
 def low_rank_step(stack, f_hi, f_lo):

time: 208 us -> 208 us (level)
  waiting for transfers between devices: 56.4 us -> 58.5 us
  transfers between devices with their start and end apart: 46 -> 46, of which waited for: 28 -> 29; matrix products, arithmetic and copies ran while one was open for 1% -> 1% of each run, Pallas kernels for 18% -> 17%
where the time goes in v3:
time: 208 us
  Pallas kernels  66.5 us (32%)
  waiting for transfers between devices  58.5 us (28%)
  starting transfers between devices  39.9 us (19%)
  blocking collectives  26.9 us (13%)
  between operations  13.9 us (7%)
    ppermute x21, waiting for transfers between devices, over_y(): lax.ppermute(value, 'tensor', along_y(d))  23.5 us
    ppermute x21, starting transfers between devices, over_y(): lax.ppermute(value, 'tensor', along_y(d))  22 us
    pallas_call x5, Pallas kernels, cg_call(): pl.pallas_call(kernel, out_shape=outs, in_specs=[VMEM] * len(operands), o...  20.1 us
    pallas_call x2, Pallas kernels, project(): pl.pallas_call(functools.partial(project_kernel, flip=flip), out_shape=ja...  14.2 us
    all_to_all x1, blocking collectives, per_device(): start_here = lax.all_to_all(start_here, 'dp', 0, 0, tiled=True)  14 us
    ppermute x3, waiting for transfers between devices, per_device(): lax.ppermute(v, 'tensor', along_y(d))  14 us
    all_to_all x1, blocking collectives, per_device(): return place_scores(lax.all_to_all(parts, 'dp', 0, 0, tiled=True))  12.9 us
    ppermute x12, waiting for transfers between devices, to_other_core(): return lax.ppermute(value, 'tensor', other_core())  12.3 us
  transfers between devices with their start and end apart: 46, of which 29 were waited for; matrix products, arithmetic and copies ran while one was open for 1% of the time, Pallas kernels for 17%

profile of v3, /device:TPU:0, one launch (start us, length us, event | category | flops | bytes accessed | tf_op | source)
XLA Modules:
  0.0 207.7 jit_solution(6152786239020956132)
XLA Ops:
  6.5 1.8 own_slab.1
  8.4 7.1 %project.3 = f32[8,256,128]{2,1,0:T(8,128)S(1)} custom-call(s32[14]{0:T(128)S(1)} %copy-done, s32[4]{0:T(128)S(1)} %copy-done.1, bf16[16,256,1792]{2,1,0:T(8,128)(2,1)} %act.3, bf16[16,256,512]{2,1,0:T(8,128)(2,1)} %grad.3, bf16[16,64,128]{2,1,0:T(8,128)(2,1)} %bitcast.3, bf16[16,64,128]{2,1,0:T(8,128)(2,1)} %bitcast.5), custom_call_target="tpu_custom_call" | custom-call | flops 2415919104 | bytes 9437184 | tf_op jit(solution)/shard_map/project/pallas_call | solution.py:133
  15.6 7.1 %project.2 = f32[8,256,128]{2,1,0:T(8,128)S(1)} custom-call(s32[14]{0:T(128)S(1)} %copy-done, s32[4]{0:T(128)S(1)} %copy-done.1, bf16[16,256,1792]{2,1,0:T(8,128)(2,1)} %act.3, bf16[16,256,512]{2,1,0:T(8,128)(2,1)} %grad.3, bf16[16,64,128]{2,1,0:T(8,128)(2,1)} %bitcast.4, bf16[16,64,128]{2,1,0:T(8,128)(2,1)} %bitcast.6), custom_call_target="tpu_custom_call" | custom-call | flops 2415919104 | bytes 9437184 | tf_op jit(solution)/shard_map/project/pallas_call | solution.py:133
  22.9 3.2 %collective-permute-start.3 = (f32[2,256,128]{2,1,0:T(8,128)S(1)}, f32[2,256,128]{2,1,0:T(8,128)S(1)}, u32[]{:S(2)}, u32[]{:S(2)}) collective-permute-start(f32[2,256,128]{2,1,0:T(8,128)S(1)} %get-tuple-element.225), channel_id=1, source_target_pairs={{0,6},{1,7},{2,0},{3,1},{4,2},{5,3},{6,4},{7,5},{8,14},{9,15},{10,... | collective-permute-start | bytes 786440 | tf_op jit(solution)/shard_map/ppermute | solution.py:615
  27.7 10.2 %collective-permute-done.3.w3 = f32[2,256,128]{2,1,0:T(8,128)S(1)} collective-permute-done((f32[2,256,128]{2,1,0:T(8,128)S(1)}, f32[2,256,128]{2,1,0:T(8,128)S(1)}, u32[]{:S(2)}, u32[]{:S(2)}) %collective-permute-start.3) | collective-permute-done | bytes 262176 | tf_op jit(solution)/shard_map/ppermute | solution.py:615
  37.9 3.7 %collective-permute-done.1.w1 = f32[2,256,128]{2,1,0:T(8,128)S(1)} collective-permute-done((f32[2,256,128]{2,1,0:T(8,128)S(1)}, f32[2,256,128]{2,1,0:T(8,128)S(1)}, u32[]{:S(2)}, u32[]{:S(2)}) %collective-permute-start.1) | collective-permute-done | bytes 262176 | tf_op jit(solution)/shard_map/ppermute | solution.py:615
  45.4 2.0 collective-permute-done.6
  47.5 2.1 %collective-permute-done.5 = f32[2,4096]{1,0:T(2,128)S(1)} collective-permute-done((f32[2,4096]{1,0:T(2,128)}, f32[2,4096]{1,0:T(2,128)S(1)}, u32[]{:S(2)}, u32[]{:S(2)}) %collective-permute-start.5) | collective-permute-done | bytes 32800 | tf_op jit(solution)/shard_map/ppermute | solution.py:588
  51.0 4.1 %collective-permute-start.9 = (f32[8,4096]{1,0:T(8,128)S(1)}, f32[8,4096]{1,0:T(8,128)S(1)}, u32[]{:S(2)}, u32[]{:S(2)}) collective-permute-start(f32[8,4096]{1,0:T(8,128)S(1)} %pad_maximum_fusion), channel_id=1, source_target_pairs={{0,24},{1,97},{2,26},{3,99},{4,28},{5,101},{6,30},{7,103},{8,0},{9... | collective-permute-start | bytes 393224 | tf_op jit(solution)/shard_map/ppermute | solution.py:588
  56.4 14.0 %all_to_all.10 = f32[16,4,256]{2,1,0:T(4,128)S(1)} all-to-all(f32[16,4,256]{2,1,0:T(4,128)S(1)} %reshape.3), channel_id=1, replica_groups=mesh['dp'=16,'tensor'=8] {'dp'}, dimensions={0} | all-to-all | bytes 131072 | tf_op jit(solution)/shard_map/all_to_all | solution.py:620
  70.4 1.8 collective-permute-start.12
  72.5 2.0 collective-permute-start.10
  75.9 2.1 collective-permute-start.16
  78.8 5.0 %collective-permute-done.16.b3 = f32[16,8,256]{2,1,0:T(8,128)S(1)} collective-permute-done((f32[16,8,256]{2,1,0:T(8,128)S(1)}, f32[16,8,256]{2,1,0:T(8,128)S(1)}, u32[]{:S(2)}, u32[]{:S(2)}) %collective-permute-start.16) | collective-permute-done | bytes 131104 | tf_op jit(solution)/shard_map/ppermute | solution.py:596
  84.7 5.7 %collective-permute-done.14.b1 = f32[16,8,256]{2,1,0:T(8,128)S(1)} collective-permute-done((f32[16,8,256]{2,1,0:T(8,128)S(1)}, f32[16,8,256]{2,1,0:T(8,128)S(1)}, u32[]{:S(2)}, u32[]{:S(2)}) %collective-permute-start.14) | collective-permute-done | bytes 131104 | tf_op jit(solution)/shard_map/ppermute | solution.py:596
  93.3 4.0 %collective-permute-done.10.n2 = f32[32,4096]{1,0:T(8,128)} collective-permute-done((f32[32,4096]{1,0:T(8,128)S(1)}, f32[32,4096]{1,0:T(8,128)}, u32[]{:S(2)}, u32[]{:S(2)}) %collective-permute-start.10) | collective-permute-done | bytes 524320 | tf_op jit(solution)/shard_map/ppermute | solution.py:588
  97.4 2.1 %collective-permute-done.19.m2 = f32[32,4096]{1,0:T(8,128)} collective-permute-done((f32[32,4096]{1,0:T(8,128)}, f32[32,4096]{1,0:T(8,128)}, u32[]{:S(2)}, u32[]{:S(2)}) %collective-permute-start.19) | collective-permute-done | bytes 524320 | tf_op jit(solution)/shard_map/ppermute | solution.py:592
  99.5 6.3 %prior_image.1 = (bf16[512,4096]{1,0:T(8,128)(2,1)S(1)}, bf16[512,4096]{1,0:T(8,128)(2,1)S(1)}, f32[40,512]{1,0:T(8,128)S(1)}) custom-call(bf16[64,4096]{1,0:T(8,128)(2,1)S(1)} %get-tuple-element.132.stack, f32[512,4096]{1,0:T(8,128)} %all-gather.2.cloned.1.call-done.prior_hbm), custom_call_target="tpu_custom_call" | custom-call | flops 3221225472 | bytes 16777216 | tf_op jit(solution)/shard_map/prior_image/pallas_call | solution.py:290
  105.8 2.8 %collective-permute-start.23 = (f32[40,512]{1,0:T(8,128)S(1)}, f32[40,512]{1,0:T(8,128)S(1)}, u32[]{:S(2)}, u32[]{:S(2)}) collective-permute-start(f32[40,512]{1,0:T(8,128)S(1)} %get-tuple-element.144), channel_id=1, source_target_pairs={{0,6},{1,7},{2,0},{3,1},{4,2},{5,3},{6,4},{7,5},{8,14},{9,15},{10,... | collective-permute-start | bytes 245768 | tf_op jit(solution)/shard_map/ppermute | solution.py:596
  110.3 4.8 %take_factors.1 = (bf16[256,4096]{1,0:T(8,128)(2,1)S(1)}, bf16[256,4096]{1,0:T(8,128)(2,1)S(1)}, f32[32,256]{1,0:T(8,128)S(1)}, f32[32,4096]{1,0:T(8,128)S(1)}, f32[8,128]{1,0:T(8,128)S(1)}) custom-call(f32[32,4096]{1,0:T(8,128)S(1)} %constant_dynamic-update-slice_fusion.n0, f32[32,4096]{1,0:T(8,128)} %copy-done.7, f32[32,4096]{1,0:T(8,128)} %collective-permute-done.10.n2, ...), custom_call_target="tpu_custom_call" | custom-call | flops 3221225472 | bytes 8388608 | tf_op jit(solution)/shard_map/take_factors/pallas_call | solution.py:339
  117.8 3.9 %first.1 = (f32[32,4096]{1,0:T(8,128)S(1)}, f32[32,4096]{1,0:T(8,128)S(1)}, bf16[64,4096]{1,0:T(8,128)(2,1)S(1)}, f32[32,128]{1,0:T(8,128)S(1)}, f32[32,256]{1,0...) custom-call(f32[40,2048]{1,0:T(8,128)S(1)} %constant_dynamic-update-slice_fusion.4.mine, ...), custom_call_target="tpu_custom_call" | custom-call | tf_op jit(solution)/shard_map/first/pallas_call | solution.py:492
  124.8 3.0 %low_rank.4 = (f32[32,256]{1,0:T(8,128)S(1)}, f32[32,4096]{1,0:T(8,128)S(1)}) custom-call(bf16[64,4096]{1,0:T(8,128)(2,1)S(1)} %get-tuple-element.155.stack, bf16[256,4096]{1,0:T(8,128)(2,1)S(1)} %get-tuple-element.156.f_hi, bf16[256,4096]{1,0:T(8,128)(2,1)S(1)} %get-tuple-element.157.f_lo), custom_call_target="tpu_custom_call" | custom-call | flops 3221225472 | bytes 4194304 | tf_op jit(solution)/shard_map/low_rank/pallas_call | solution.py:357
  127.8 1.8 collective-permute-done.26
  131.9 4.0 %step.3 = (f32[32,4096]{1,0:T(8,128)S(1)}, f32[32,4096]{1,0:T(8,128)S(1)}, bf16[64,4096]{1,0:T(8,128)(2,1)S(1)}, f32[32,128]{1,0:T(8,128)S(1)}, f32[32,256]{1,0:T(8,128)S(1)}, /*index=5*/f32[32,512]{1,0:T(8,128)S(1)}) custom-call(f32[32,2048]{1,0:T(8,128)S(1)} %constant_dynamic-update-slice_fusion.8.mine, f32[32,2048]{1,0:T(8,128)S(1)} %collective-permute-done.28.theirs, ...), custom_call_target="tpu_custom_call" | custom-call | tf_op jit(solution)/shard_map/step/pallas_call | solution.py:492
  138.6 3.0 %low_rank.5 = (f32[32,256]{1,0:T(8,128)S(1)}, f32[32,4096]{1,0:T(8,128)S(1)}) custom-call(bf16[64,4096]{1,0:T(8,128)(2,1)S(1)} %get-tuple-element.172.stack, bf16[256,4096]{1,0:T(8,128)(2,1)S(1)} %get-tuple-element.156.f_hi, bf16[256,4096]{1,0:T(8,128)(2,1)S(1)} %get-tuple-element.157.f_lo), custom_call_target="tpu_custom_call" | custom-call | flops 3221225472 | bytes 4194304 | tf_op jit(solution)/shard_map/low_rank/pallas_call | solution.py:357
  145.4 4.0 %step.4 = (f32[32,4096]{1,0:T(8,128)S(1)}, f32[32,4096]{1,0:T(8,128)S(1)}, bf16[64,4096]{1,0:T(8,128)(2,1)S(1)}, f32[32,128]{1,0:T(8,128)S(1)}, f32[32,256]{1,0:T(8,128)S(1)}, /*index=5*/f32[32,512]{1,0:T(8,128)S(1)}) custom-call(f32[32,2048]{1,0:T(8,128)S(1)} %constant_dynamic-update-slice_fusion.12.mine, f32[32,2048]{1,0:T(8,128)S(1)} %collective-permute-done.32.theirs, ...), custom_call_target="tpu_custom_call" | custom-call | tf_op jit(solution)/shard_map/step/pallas_call | solution.py:492
  152.5 3.0 %low_rank.6 = (f32[32,256]{1,0:T(8,128)S(1)}, f32[32,4096]{1,0:T(8,128)S(1)}) custom-call(bf16[64,4096]{1,0:T(8,128)(2,1)S(1)} %get-tuple-element.186.stack, bf16[256,4096]{1,0:T(8,128)(2,1)S(1)} %get-tuple-element.156.f_hi, bf16[256,4096]{1,0:T(8,128)(2,1)S(1)} %get-tuple-element.157.f_lo), custom_call_target="tpu_custom_call" | custom-call | flops 3221225472 | bytes 4194304 | tf_op jit(solution)/shard_map/low_rank/pallas_call | solution.py:357
  159.3 4.0 %step.5 = (f32[32,4096]{1,0:T(8,128)S(1)}, f32[32,4096]{1,0:T(8,128)S(1)}, bf16[64,4096]{1,0:T(8,128)(2,1)S(1)}, f32[32,128]{1,0:T(8,128)S(1)}, f32[32,256]{1,0:T(8,128)S(1)}, /*index=5*/f32[32,512]{1,0:T(8,128)S(1)}) custom-call(f32[32,2048]{1,0:T(8,128)S(1)} %constant_dynamic-update-slice_fusion.16.mine, f32[32,2048]{1,0:T(8,128)S(1)} %collective-permute-done.36.theirs, ...), custom_call_target="tpu_custom_call" | custom-call | tf_op jit(solution)/shard_map/step/pallas_call | solution.py:492
  165.8 3.0 %low_rank.7 = (f32[32,256]{1,0:T(8,128)S(1)}, f32[32,4096]{1,0:T(8,128)S(1)}) custom-call(bf16[64,4096]{1,0:T(8,128)(2,1)S(1)} %get-tuple-element.200.stack, bf16[256,4096]{1,0:T(8,128)(2,1)S(1)} %get-tuple-element.156.f_hi, bf16[256,4096]{1,0:T(8,128)(2,1)S(1)} %get-tuple-element.157.f_lo), custom_call_target="tpu_custom_call" | custom-call | flops 3221225472 | bytes 4194304 | tf_op jit(solution)/shard_map/low_rank/pallas_call | solution.py:357
  172.5 4.3 %last.1 = (bf16[64,4096]{1,0:T(8,128)(2,1)S(1)}, f32[32,128]{1,0:T(8,128)S(1)}, f32[32,256]{1,0:T(8,128)S(1)}, f32[32,128]{1,0:T(8,128)S(1)}, f32[32,128]{1,0:T(8,128)S(1)}) custom-call(f32[32,2048]{1,0:T(8,128)S(1)} %constant_dynamic-update-slice_fusion.20.mine, f32[32,2048]{1,0:T(8,128)S(1)} %collective-permute-done.40.theirs, ...), custom_call_target="tpu_custom_call" | custom-call | tf_op jit(solution)/shard_map/last/pallas_call | solution.py:492
  179.9 2.0 last_query.1
  186.3 12.9 %all_to_all.11.parts = f32[16,8,128]{2,1,0:T(8,128)} all-to-all(f32[16,8,128]{2,1,0:T(8,128)} %finish.1), channel_id=1, replica_groups=mesh['dp'=16,'tensor'=8] {'dp'}, dimensions={0} | all-to-all | bytes 131072 | tf_op jit(solution)/shard_map/all_to_all | solution.py:672
  (127 shorter events, 53.1 us)
Async XLA Ops:
  6.5 93.0 %all-gather.2.cloned.1.call-start = ((), (), s32[]{:S(2)}) async-start(), calls=%async_computation.2 | async-start | bytes 8912896 | tf_op jit(solution)/shard_map/all_gather | solution.py:608
  15.5 7.2 %collective-permute-start = (f32[8,256,128]{2,1,0:T(8,128)S(1)}, f32[8,256,128]{2,1,0:T(8,128)S(1)}, u32[]{:S(2)}, u32[]{:S(2)}) collective-permute-start(f32[8,256,128]{2,1,0:T(8,128)S(1)} %project.3), channel_id=1, source_target_pairs={{0,1},{1,0},{2,3},{3,2},{4,5},{5,4},{6,7},{7,6},{8,9},{9,8},{10,11... | collective-permute-start | bytes 3145736 | tf_op jit(solution)/shard_map/ppermute | solution.py:592
  22.9 15.0 %collective-permute-start.3 = (f32[2,256,128]{2,1,0:T(8,128)S(1)}, f32[2,256,128]{2,1,0:T(8,128)S(1)}, u32[]{:S(2)}, u32[]{:S(2)}) collective-permute-start(f32[2,256,128]{2,1,0:T(8,128)S(1)} %get-tuple-element.225), channel_id=1, source_target_pairs={{0,6},{1,7},{2,0},{3,1},{4,2},{5,3},{6,4},{7,5},{8,14},{9,15},{10,... | collective-permute-start | bytes 786440 | tf_op jit(solution)/shard_map/ppermute | solution.py:615
  26.1 11.8 %collective-permute-start.2 = (f32[2,256,128]{2,1,0:T(8,128)S(1)}, f32[2,256,128]{2,1,0:T(8,128)S(1)}, u32[]{:S(2)}, u32[]{:S(2)}) collective-permute-start(f32[2,256,128]{2,1,0:T(8,128)S(1)} %get-tuple-element.226), channel_id=1, source_target_pairs={{0,4},{1,5},{2,6},{3,7},{4,0},{5,1},{6,2},{7,3},{8,12},{9,13},{10,... | collective-permute-start | bytes 786440 | tf_op jit(solution)/shard_map/ppermute | solution.py:615
  26.7 14.9 %collective-permute-start.1 = (f32[2,256,128]{2,1,0:T(8,128)S(1)}, f32[2,256,128]{2,1,0:T(8,128)S(1)}, u32[]{:S(2)}, u32[]{:S(2)}) collective-permute-start(f32[2,256,128]{2,1,0:T(8,128)S(1)} %get-tuple-element.227), channel_id=1, source_target_pairs={{0,2},{1,3},{2,4},{3,5},{4,6},{5,7},{6,0},{7,1},{8,10},{9,11},{10,... | collective-permute-start | bytes 786440 | tf_op jit(solution)/shard_map/ppermute | solution.py:615
  44.0 5.7 %collective-permute-start.5 = (f32[2,4096]{1,0:T(2,128)}, f32[2,4096]{1,0:T(2,128)S(1)}, u32[]{:S(2)}, u32[]{:S(2)}) collective-permute-start(f32[2,4096]{1,0:T(2,128)} %factor.1), channel_id=1, source_target_pairs={{0,4},{1,5},{2,6},{3,7},{4,0},{5,1},{6,2},{7,3},{8,12},{9,13},{10,... | collective-permute-start | bytes 98312 | tf_op jit(solution)/shard_map/ppermute | solution.py:588
  44.6 5.6 %collective-permute-start.4 = (f32[2,4096]{1,0:T(2,128)}, f32[2,4096]{1,0:T(2,128)S(1)}, u32[]{:S(2)}, u32[]{:S(2)}) collective-permute-start(f32[2,4096]{1,0:T(2,128)} %factor.1), channel_id=1, source_target_pairs={{0,2},{1,3},{2,4},{3,5},{4,6},{5,7},{6,0},{7,1},{8,10},{9,11},{10,... | collective-permute-start | bytes 98312 | tf_op jit(solution)/shard_map/ppermute | solution.py:588
  51.0 19.3 %collective-permute-start.9 = (f32[8,4096]{1,0:T(8,128)S(1)}, f32[8,4096]{1,0:T(8,128)S(1)}, u32[]{:S(2)}, u32[]{:S(2)}) collective-permute-start(f32[8,4096]{1,0:T(8,128)S(1)} %pad_maximum_fusion), channel_id=1, source_target_pairs={{0,24},{1,97},{2,26},{3,99},{4,28},{5,101},{6,30},{7,103},{8,0},{9... | collective-permute-start | bytes 393224 | tf_op jit(solution)/shard_map/ppermute | solution.py:588
  55.1 15.2 %collective-permute-start.8 = (f32[8,4096]{1,0:T(8,128)S(1)}, f32[8,4096]{1,0:T(8,128)S(1)}, u32[]{:S(2)}, u32[]{:S(2)}) collective-permute-start(f32[8,4096]{1,0:T(8,128)S(1)} %pad_maximum_fusion), channel_id=1, source_target_pairs={{0,16},{1,65},{2,18},{3,67},{4,20},{5,69},{6,22},{7,71},{8,24},{9,... | collective-permute-start | bytes 393224 | tf_op jit(solution)/shard_map/ppermute | solution.py:588
  55.1 15.2 %collective-permute-start.7 = (f32[8,4096]{1,0:T(8,128)S(1)}, f32[8,4096]{1,0:T(8,128)S(1)}, u32[]{:S(2)}, u32[]{:S(2)}) collective-permute-start(f32[8,4096]{1,0:T(8,128)S(1)} %pad_maximum_fusion), channel_id=1, source_target_pairs={{0,8},{1,33},{2,10},{3,35},{4,12},{5,37},{6,14},{7,39},{8,16},{9,4... | collective-permute-start | bytes 393224 | tf_op jit(solution)/shard_map/ppermute | solution.py:588
  70.4 20.0 %collective-permute-start.12 = (f32[32,4096]{1,0:T(8,128)S(1)}, f32[32,4096]{1,0:T(8,128)}, u32[]{:S(2)}, u32[]{:S(2)}) collective-permute-start(f32[32,4096]{1,0:T(8,128)S(1)} %constant_dynamic-update-slice_fusion.n0), channel_id=1, source_target_pairs={{0,96},{1,25},{2,98},{3,27},{4,100},{5,29},{6,102},{7,31},{8,104},... | collective-permute-start | bytes 1572872 | tf_op jit(solution)/shard_map/ppermute | solution.py:588
  72.3 20.1 %collective-permute-start.11 = (f32[32,4096]{1,0:T(8,128)S(1)}, f32[32,4096]{1,0:T(8,128)S(1)}, u32[]{:S(2)}, u32[]{:S(2)}) collective-permute-start(f32[32,4096]{1,0:T(8,128)S(1)} %constant_dynamic-update-slice_fusion.n0), channel_id=1, source_target_pairs={{0,32},{1,9},{2,34},{3,11},{4,36},{5,13},{6,38},{7,15},{8,40},{9,1... | collective-permute-start | bytes 1572872 | tf_op jit(solution)/shard_map/ppermute | solution.py:588
  72.5 24.7 %collective-permute-start.10 = (f32[32,4096]{1,0:T(8,128)S(1)}, f32[32,4096]{1,0:T(8,128)}, u32[]{:S(2)}, u32[]{:S(2)}) collective-permute-start(f32[32,4096]{1,0:T(8,128)S(1)} %constant_dynamic-update-slice_fusion.n0), channel_id=1, source_target_pairs={{0,64},{1,17},{2,66},{3,19},{4,68},{5,21},{6,70},{7,23},{8,72},{9,... | collective-permute-start | bytes 1572872 | tf_op jit(solution)/shard_map/ppermute | solution.py:588
  75.9 8.0 %collective-permute-start.16 = (f32[16,8,256]{2,1,0:T(8,128)S(1)}, f32[16,8,256]{2,1,0:T(8,128)S(1)}, u32[]{:S(2)}, u32[]{:S(2)}) collective-permute-start(f32[16,8,256]{2,1,0:T(8,128)S(1)} %maximum_select_fusion.b0), channel_id=1, source_target_pairs={{0,6},{1,7},{2,0},{3,1},{4,2},{5,3},{6,4},{7,5},{8,14},{9,15},{10,... | collective-permute-start | bytes 393224 | tf_op jit(solution)/shard_map/ppermute | solution.py:596
  77.9 6.8 %collective-permute-start.15 = (f32[16,8,256]{2,1,0:T(8,128)S(1)}, f32[16,8,256]{2,1,0:T(8,128)S(1)}, u32[]{:S(2)}, u32[]{:S(2)}) collective-permute-start(f32[16,8,256]{2,1,0:T(8,128)S(1)} %maximum_select_fusion.b0), channel_id=1, source_target_pairs={{0,4},{1,5},{2,6},{3,7},{4,0},{5,1},{6,2},{7,3},{8,12},{9,13},{10,... | collective-permute-start | bytes 393224 | tf_op jit(solution)/shard_map/ppermute | solution.py:596
  83.8 6.6 %collective-permute-start.14 = (f32[16,8,256]{2,1,0:T(8,128)S(1)}, f32[16,8,256]{2,1,0:T(8,128)S(1)}, u32[]{:S(2)}, u32[]{:S(2)}) collective-permute-start(f32[16,8,256]{2,1,0:T(8,128)S(1)} %maximum_select_fusion.b0), channel_id=1, source_target_pairs={{0,2},{1,3},{2,4},{3,5},{4,6},{5,7},{6,0},{7,1},{8,10},{9,11},{10,... | collective-permute-start | bytes 393224 | tf_op jit(solution)/shard_map/ppermute | solution.py:596
  90.4 6.9 %collective-permute-start.17 = (f32[32,4096]{1,0:T(8,128)S(1)}, f32[32,4096]{1,0:T(8,128)S(1)}, u32[]{:S(2)}, u32[]{:S(2)}) collective-permute-start(f32[32,4096]{1,0:T(8,128)S(1)} %constant_dynamic-update-slice_fusion.n0), channel_id=1, source_target_pairs={{0,1},{1,0},{2,3},{3,2},{4,5},{5,4},{6,7},{7,6},{8,9},{9,8},{10,11... | collective-permute-start | bytes 1572872 | tf_op jit(solution)/shard_map/ppermute | solution.py:592
  90.5 6.9 %collective-permute-start.20 = (f32[32,4096]{1,0:T(8,128)}, f32[32,4096]{1,0:T(8,128)S(1)}, u32[]{:S(2)}, u32[]{:S(2)}) collective-permute-start(f32[32,4096]{1,0:T(8,128)} %collective-permute-done.12.n3), channel_id=1, source_target_pairs={{0,1},{1,0},{2,3},{3,2},{4,5},{5,4},{6,7},{7,6},{8,9},{9,8},{10,11... | collective-permute-start | bytes 1572872 | tf_op jit(solution)/shard_map/ppermute | solution.py:592
  105.8 9.3 %collective-permute-start.23 = (f32[40,512]{1,0:T(8,128)S(1)}, f32[40,512]{1,0:T(8,128)S(1)}, u32[]{:S(2)}, u32[]{:S(2)}) collective-permute-start(f32[40,512]{1,0:T(8,128)S(1)} %get-tuple-element.144), channel_id=1, source_target_pairs={{0,6},{1,7},{2,0},{3,1},{4,2},{5,3},{6,4},{7,5},{8,14},{9,15},{10,... | collective-permute-start | bytes 245768 | tf_op jit(solution)/shard_map/ppermute | solution.py:596
  108.6 6.6 %collective-permute-start.22 = (f32[40,512]{1,0:T(8,128)S(1)}, f32[40,512]{1,0:T(8,128)S(1)}, u32[]{:S(2)}, u32[]{:S(2)}) collective-permute-start(f32[40,512]{1,0:T(8,128)S(1)} %get-tuple-element.144), channel_id=1, source_target_pairs={{0,4},{1,5},{2,6},{3,7},{4,0},{5,1},{6,2},{7,3},{8,12},{9,13},{10,... | collective-permute-start | bytes 245768 | tf_op jit(solution)/shard_map/ppermute | solution.py:596
  109.4 6.7 %collective-permute-start.21 = (f32[40,512]{1,0:T(8,128)S(1)}, f32[40,512]{1,0:T(8,128)S(1)}, u32[]{:S(2)}, u32[]{:S(2)}) collective-permute-start(f32[40,512]{1,0:T(8,128)S(1)} %get-tuple-element.144), channel_id=1, source_target_pairs={{0,2},{1,3},{2,4},{3,5},{4,6},{5,7},{6,0},{7,1},{8,10},{9,11},{10,... | collective-permute-start | bytes 245768 | tf_op jit(solution)/shard_map/ppermute | solution.py:596
  121.8 5.9 %collective-permute-start.27 = (f32[32,512]{1,0:T(8,128)S(1)}, f32[32,512]{1,0:T(8,128)S(1)}, u32[]{:S(2)}, u32[]{:S(2)}) collective-permute-start(f32[32,512]{1,0:T(8,128)S(1)} %get-tuple-element.160), channel_id=1, source_target_pairs={{0,6},{1,7},{2,0},{3,1},{4,2},{5,3},{6,4},{7,5},{8,14},{9,15},{10,... | collective-permute-start | bytes 196616 | tf_op jit(solution)/shard_map/ppermute | solution.py:596
  123.3 6.3 %collective-permute-start.26 = (f32[32,512]{1,0:T(8,128)S(1)}, f32[32,512]{1,0:T(8,128)S(1)}, u32[]{:S(2)}, u32[]{:S(2)}) collective-permute-start(f32[32,512]{1,0:T(8,128)S(1)} %get-tuple-element.160), channel_id=1, source_target_pairs={{0,4},{1,5},{2,6},{3,7},{4,0},{5,1},{6,2},{7,3},{8,12},{9,13},{10,... | collective-permute-start | bytes 196616 | tf_op jit(solution)/shard_map/ppermute | solution.py:596
  124.8 5.5 %collective-permute-start.25 = (f32[32,512]{1,0:T(8,128)S(1)}, f32[32,512]{1,0:T(8,128)S(1)}, u32[]{:S(2)}, u32[]{:S(2)}) collective-permute-start(f32[32,512]{1,0:T(8,128)S(1)} %get-tuple-element.160), channel_id=1, source_target_pairs={{0,2},{1,3},{2,4},{3,5},{4,6},{5,7},{6,0},{7,1},{8,10},{9,11},{10,... | collective-permute-start | bytes 196616 | tf_op jit(solution)/shard_map/ppermute | solution.py:596
  135.9 5.7 %collective-permute-start.31 = (f32[32,512]{1,0:T(8,128)S(1)}, f32[32,512]{1,0:T(8,128)S(1)}, u32[]{:S(2)}, u32[]{:S(2)}) collective-permute-start(f32[32,512]{1,0:T(8,128)S(1)} %get-tuple-element.175), channel_id=1, source_target_pairs={{0,6},{1,7},{2,0},{3,1},{4,2},{5,3},{6,4},{7,5},{8,14},{9,15},{10,... | collective-permute-start | bytes 196616 | tf_op jit(solution)/shard_map/ppermute | solution.py:596
  136.7 6.0 %collective-permute-start.30 = (f32[32,512]{1,0:T(8,128)S(1)}, f32[32,512]{1,0:T(8,128)S(1)}, u32[]{:S(2)}, u32[]{:S(2)}) collective-permute-start(f32[32,512]{1,0:T(8,128)S(1)} %get-tuple-element.175), channel_id=1, source_target_pairs={{0,4},{1,5},{2,6},{3,7},{4,0},{5,1},{6,2},{7,3},{8,12},{9,13},{10,... | collective-permute-start | bytes 196616 | tf_op jit(solution)/shard_map/ppermute | solution.py:596
  137.8 5.7 %collective-permute-start.29 = (f32[32,512]{1,0:T(8,128)S(1)}, f32[32,512]{1,0:T(8,128)S(1)}, u32[]{:S(2)}, u32[]{:S(2)}) collective-permute-start(f32[32,512]{1,0:T(8,128)S(1)} %get-tuple-element.175), channel_id=1, source_target_pairs={{0,2},{1,3},{2,4},{3,5},{4,6},{5,7},{6,0},{7,1},{8,10},{9,11},{10,... | collective-permute-start | bytes 196616 | tf_op jit(solution)/shard_map/ppermute | solution.py:596
  149.3 6.1 %collective-permute-start.35 = (f32[32,512]{1,0:T(8,128)S(1)}, f32[32,512]{1,0:T(8,128)S(1)}, u32[]{:S(2)}, u32[]{:S(2)}) collective-permute-start(f32[32,512]{1,0:T(8,128)S(1)} %get-tuple-element.189), channel_id=1, source_target_pairs={{0,6},{1,7},{2,0},{3,1},{4,2},{5,3},{6,4},{7,5},{8,14},{9,15},{10,... | collective-permute-start | bytes 196616 | tf_op jit(solution)/shard_map/ppermute | solution.py:596
  150.9 6.3 %collective-permute-start.34 = (f32[32,512]{1,0:T(8,128)S(1)}, f32[32,512]{1,0:T(8,128)S(1)}, u32[]{:S(2)}, u32[]{:S(2)}) collective-permute-start(f32[32,512]{1,0:T(8,128)S(1)} %get-tuple-element.189), channel_id=1, source_target_pairs={{0,4},{1,5},{2,6},{3,7},{4,0},{5,1},{6,2},{7,3},{8,12},{9,13},{10,... | collective-permute-start | bytes 196616 | tf_op jit(solution)/shard_map/ppermute | solution.py:596
  151.8 5.9 %collective-permute-start.33 = (f32[32,512]{1,0:T(8,128)S(1)}, f32[32,512]{1,0:T(8,128)S(1)}, u32[]{:S(2)}, u32[]{:S(2)}) collective-permute-start(f32[32,512]{1,0:T(8,128)S(1)} %get-tuple-element.189), channel_id=1, source_target_pairs={{0,2},{1,3},{2,4},{3,5},{4,6},{5,7},{6,0},{7,1},{8,10},{9,11},{10,... | collective-permute-start | bytes 196616 | tf_op jit(solution)/shard_map/ppermute | solution.py:596
  164.1 6.0 %collective-permute-start.38 = (f32[32,512]{1,0:T(8,128)S(1)}, f32[32,512]{1,0:T(8,128)S(1)}, u32[]{:S(2)}, u32[]{:S(2)}) collective-permute-start(f32[32,512]{1,0:T(8,128)S(1)} %get-tuple-element.203), channel_id=1, source_target_pairs={{0,4},{1,5},{2,6},{3,7},{4,0},{5,1},{6,2},{7,3},{8,12},{9,13},{10,... | collective-permute-start | bytes 196616 | tf_op jit(solution)/shard_map/ppermute | solution.py:596
  165.1 5.7 %collective-permute-start.37 = (f32[32,512]{1,0:T(8,128)S(1)}, f32[32,512]{1,0:T(8,128)S(1)}, u32[]{:S(2)}, u32[]{:S(2)}) collective-permute-start(f32[32,512]{1,0:T(8,128)S(1)} %get-tuple-element.203), channel_id=1, source_target_pairs={{0,2},{1,3},{2,4},{3,5},{4,6},{5,7},{6,0},{7,1},{8,10},{9,11},{10,... | collective-permute-start | bytes 196616 | tf_op jit(solution)/shard_map/ppermute | solution.py:596
  (22 other events, 98.7 us)
Sparse Core Ops, SparseCore 0:
  9.5 83.0 all-gather.1
